TPU v7x, 32 devices: a whole 2x2x4 slice. The times are simulated.
32 devices in a mesh: tile: 4 (over z), lat: 4 (over y, x), emu: 2 (over core).
Axes of the slice: x: 2, y: 2, z: 4, core: 2. Of those that a mesh axis runs over, the one named last changes fastest.
Arguments:
- state: float32 [64, 128, 12, 128], P('tile', ('lat', 'emu')), may hold values from -6 to 6
- diffusivity: float32 [12, 128], replicated, may hold values from 0.03 to 0.2
- wind: float32 [64, 128], P('tile', ('lat', 'emu')), may hold values from -0.5 to 0.5
- land_mask: int32 [64, 128], P('tile', ('lat', 'emu')), may hold values 0 or 1
- routes: int32 [4, 4, 2, 256, 1], P('tile', 'lat', 'emu'), may hold values from 0 to 15; in each aligned block of 256 rows (0 to 255, 256 to 511, ..., all dimensions but the last counted through in order) at most 20 rows name the same one
- counts: int32 [4, 4, 2], P('tile', 'lat', 'emu'), may hold values from 64 to 256
- w_in: bfloat16 [16, 1536, 1024], P(('tile', 'lat')), may hold values from -0.15625 to 0.15625
- b_in: float32 [16, 1024], P(('tile', 'lat')), may hold values from -3 to 3
- land_vec: float32 [16, 1024], P(('tile', 'lat')), may hold values from -5 to 5
- w_hid: bfloat16 [16, 2, 1024, 1024], P(('tile', 'lat')), may hold values from -0.1875 to 0.1875
- b_hid: float32 [16, 2, 1024], P(('tile', 'lat')), may hold values from -3 to 3
- w_out: bfloat16 [16, 1024, 512], P(('tile', 'lat')), may hold values from -0.1875 to 0.1875
Outputs:
- updated: float32 [64, 128, 4, 128], P('tile', ('lat', 'emu'))
Inputs may be any that keep to these rules, and one draw needn't show every extreme that they name: `routes`: among the 256 columns of one device, at most 20 name the same expert.
All inputs are finite; a program needn't handle non-finite values. No bound on the sum of `land_mask` on one device may be relied on, other than what follows from the above.
Results may differ from a plain program's by a relative error of at most 0.0026.
Values may be sent and summed in bfloat16 or wider, within the bound.
No kernel may reach another device: no remote copies, remote signals or barrier semaphores. Data moves between devices by JAX's collectives and lax.ppermute only.
A program may use at most 64 MiB of HBM per device.

v0:
```python
import jax
import jax.numpy as jnp
from jax import lax
from jax.sharding import PartitionSpec as P


def extended(block, sides, width, periodic):
    for axis, dim in sides:
        count = lax.axis_size(axis)
        forward = [(i, i + 1) for i in range(count - 1)]
        if periodic:
            forward.append((count - 1, 0))
        backward = [(target, source) for source, target in forward]
        low = lax.ppermute(
            lax.slice_in_dim(block, block.shape[dim] - width, None, axis=dim), axis, forward
        )
        high = lax.ppermute(lax.slice_in_dim(block, 0, width, axis=dim), axis, backward)
        block = jnp.concatenate([low, block, high], axis=dim)
    return block


def advance(center, east, west, north, south, diffusivity, wind):
    spread = east + west + north + south - 4.0 * center
    return center + diffusivity[None, None] * spread - 0.5 * wind[:, :, None, None] * (east - west)


def column_slots(route_flat, count, experts, capacity):
    columns = route_flat.shape[0]
    positions = jnp.arange(columns, dtype=jnp.int32)
    active = positions < count
    onehot = (
        (route_flat[:, None] == jnp.arange(experts, dtype=jnp.int32)[None, :]) & active[:, None]
    ).astype(jnp.int32)
    before = jnp.cumsum(onehot, axis=0) - onehot
    ranking = jnp.sum(before * onehot, axis=1)
    slot_index = jnp.where(active, route_flat * capacity + ranking, experts * capacity)
    return (slot_index, active)


def run_network(features, flags, w_first, b_first, land_add, w_inner, b_inner, w_last):
    lead = features.shape[:-1]
    rows = features.reshape(-1, features.shape[-1])
    pre = jnp.dot(rows, w_first, preferred_element_type=jnp.float32) + b_first[None, :]
    pre = pre + flags.reshape(-1, 1).astype(jnp.float32) * land_add[None, :]
    hidden = jax.nn.silu(pre).astype(jnp.bfloat16)
    for number in range(w_inner.shape[0]):
        inner = (
            jnp.dot(hidden, w_inner[number], preferred_element_type=jnp.float32)
            + b_inner[number][None, :]
        )
        hidden = jax.nn.silu(inner).astype(jnp.bfloat16)
    produced = jnp.dot(hidden, w_last, preferred_element_type=jnp.float32).astype(jnp.bfloat16)
    return produced.reshape(lead + (w_last.shape[1],))


def body(
    state, diffusivity, wind, land_mask, routes, counts, w_in, b_in, land_vec, w_hid, b_hid, w_out
):
    lon_cells, lat_cells, variables, levels = state.shape
    lon_ext = extended(state, (("tile", 0),), 1, True)
    lat_ext = extended(state, ((("lat", "emu"), 1),), 1, False)
    advanced = advance(
        state, lon_ext[2:], lon_ext[:-2], lat_ext[:, 2:], lat_ext[:, :-2], diffusivity, wind
    )
    columns = lon_cells * lat_cells
    fsize = variables * levels
    outf = w_out.shape[2]
    out_vars = outf // levels
    tiles = lax.axis_size("tile")
    bands = lax.axis_size("lat")
    experts = tiles * bands
    capacity = max(2, columns * 5 // (4 * experts))
    features = advanced.astype(jnp.bfloat16).reshape(columns, fsize)
    slot_index, active = column_slots(
        routes.reshape(columns), counts.reshape(()), experts, capacity
    )
    outbound = jnp.zeros((experts * capacity + 1, fsize), jnp.bfloat16).at[slot_index].set(features)
    outbound = outbound[:-1].reshape(experts, capacity, fsize)
    land_rows = land_mask.reshape(columns, 1).astype(jnp.bfloat16)
    flags = jnp.zeros((experts * capacity + 1, 1), jnp.bfloat16).at[slot_index].set(land_rows)
    flags = flags[:-1].reshape(experts, capacity, 1)
    produced = run_network(
        lax.all_to_all(outbound, ("tile", "lat"), split_axis=0, concat_axis=0, tiled=True),
        lax.all_to_all(flags, ("tile", "lat"), split_axis=0, concat_axis=0, tiled=True),
        w_in[0],
        b_in[0],
        land_vec[0],
        w_hid[0],
        b_hid[0],
        w_out[0],
    )
    returned = lax.all_to_all(produced, ("tile", "lat"), split_axis=0, concat_axis=0, tiled=True)
    flat = jnp.concatenate([returned.reshape(-1, outf), jnp.zeros((1, outf), jnp.bfloat16)], axis=0)
    tendency = flat[slot_index].astype(jnp.float32)
    return advanced[:, :, :out_vars, :] + tendency.reshape(lon_cells, lat_cells, out_vars, levels)


def solution(mesh):
    in_specs = (
        P("tile", ("lat", "emu"), None, None),
        P(),
        P("tile", ("lat", "emu")),
        P("tile", ("lat", "emu")),
        P("tile", "lat", "emu", None, None),
        P("tile", "lat", "emu"),
        P(("tile", "lat"), None, None),
        P(("tile", "lat"), None),
        P(("tile", "lat"), None),
        P(("tile", "lat"), None, None, None),
        P(("tile", "lat"), None, None),
        P(("tile", "lat"), None, None),
    )
    out_specs = P("tile", ("lat", "emu"), None, None)
    return jax.shard_map(body, mesh=mesh, in_specs=in_specs, out_specs=out_specs, check_vma=False)
```

profile of v0, /device:TPU:0, one launch (start us, length us, event | category | flops | bytes accessed | tf_op | source)
XLA Modules:
  0.0 119.9 jit_solution(5788248250496178176)
XLA Ops:
  0.0 0.0 copy-start
  0.0 0.0 copy-start.2
  0.0 2.1 %copy.43 = f32[16,16,12,128]{3,2,1,0:T(8,128)S(1)} copy(f32[16,16,12,128]{3,1,2,0:T(8,128)} %param.12) | data formatting | bytes 3145728 | tf_op args[0]
  2.1 0.0 copy-start.1
  2.1 0.8 fusion.59
  2.9 5.1 %collective-permute-start = (f32[1,16,12,128]{3,2,1,0:T(8,128)}, f32[1,16,12,128]{3,2,1,0:T(8,128)S(1)}, u32[]{:S(2)}, u32[]{:S(2)}) collective-permute-start(f32[1,16,12,128]{3,2,1,0:T(8,128)} %get-tuple-element.7), channel_id=1, source_target_pairs={{8,0},{16,8},{24,16},{0,24},{9,1},{17,9},{25,17},{1,25},{10,2},{18... | collective-permute-start | bytes 294920 | tf_op jit(solution)/shard_map/ppermute | solution.py:17
  7.9 0.0 collective-permute-start.1
  7.9 0.0 copy-done.1
  7.9 0.7 fusion.60
  8.7 1.3 %collective-permute-start.2 = (f32[16,1,12,128]{3,2,1,0:T(8,128)}, f32[16,1,12,128]{3,2,1,0:T(8,128)S(1)}, u32[]{:S(2)}, u32[]{:S(2)}) collective-permute-start(f32[16,1,12,128]{3,2,1,0:T(8,128)} %get-tuple-element.9), channel_id=1, source_target_pairs={{1,0},{2,1},{3,2},{4,3},{5,4},{6,5},{7,6},{9,8},{10,9},{11,10},{12... | collective-permute-start | bytes 294920 | tf_op jit(solution)/shard_map/ppermute | solution.py:17
  9.9 3.7 %collective-permute-start.3 = (f32[16,1,12,128]{3,2,1,0:T(8,128)}, f32[16,1,12,128]{3,2,1,0:T(8,128)}, u32[]{:S(2)}, u32[]{:S(2)}) collective-permute-start(f32[16,1,12,128]{3,2,1,0:T(8,128)} %get-tuple-element.10), channel_id=1, source_target_pairs={{0,1},{1,2},{2,3},{3,4},{4,5},{5,6},{6,7},{8,9},{9,10},{10,11},{11... | collective-permute-start | bytes 294920 | tf_op jit(solution)/shard_map/ppermute | solution.py:14
  14.3 0.0 copy-done.2
  14.3 0.6 fusion.52
  14.9 1.3 %reduce-window.6 = s32[16,2,128]{2,0,1:T(8,128)S(1)} reduce-window(s32[16,2,128]{2,0,1:T(8,128)} %fusion.52, s32[]{:T(128)} %constant.24.clone.1), window={size=1x1x128 pad=0_0x0_0x127_0}, to_apply=%region_0.0 | reduce-window | flops 520192 | bytes 32772 | tf_op jit(solution)/shard_map/reduce-window
  16.2 0.8 slice_reduce_fusion
  16.9 1.3 %reduce-window.9 = s32[16,3]{0,1:T(4,128)} reduce-window(s32[16,2]{0,1:T(2,128)} %slice_reduce_fusion, s32[]{:T(128)} %constant.24.clone.1), window={size=1x2 pad=0_0x2_0}, to_apply=%region_1.2 | reduce-window | flops 48 | bytes 324 | tf_op jit(solution)/shard_map/reduce-window.1
  18.2 1.2 %slice.69 = s32[16,2]{0,1:T(2,128)} slice(s32[16,3]{0,1:T(4,128)} %reduce-window.9), slice={[0:16], [0:2]} | slice | bytes 256 | tf_op jit(solution)/shard_map/slice.1
  19.4 0.6 iota_compare_fusion.2
  20.0 1.3 %convert_element_type.57 = bf16[16,16]{1,0:T(8,128)(2,1)} convert(s32[16,16]{1,0:T(8,128)} %param.15) | non-fusion elementwise | flops 256 | bytes 1536 | tf_op jit(solution)/shard_map/convert_element_type | solution.py:79
  21.3 1.3 %reshape.156 = bf16[256]{0:T(256)(128)(2,1)} reshape(bf16[16,16]{1,0:T(8,128)(2,1)} %convert_element_type.57) | data formatting | bytes 1024 | tf_op jit(solution)/shard_map/convert_element_type | solution.py:79
  22.7 0.8 fusion.49
  23.4 0.7 compare_select_fusion
  24.1 0.0 copy-start.4
  24.1 2.3 %scatter_custom_fusion.1 = bf16[321]{0:T(512)(128)(2,1)S(1)} fusion(s32[256]{0:T(256)S(1)} %bitcast.76, bf16[256]{0:T(256)(128)(2,1)} %reshape.156, bf16[]{:T(256)} %constant.7.clone.1), kind=kCustom, calls=%fused_computation.60 | custom fusion | bytes 1154 | tf_op jit(solution)/shard_map/scatter | solution.py:80
  26.4 0.7 reshape.163
  27.1 6.5 %all-to-all-start.1 = ((bf16[16,20,1]{1,2,0:T(2,128)(2,1)}), bf16[16,20,1]{1,2,0:T(2,128)(2,1)S(1)}, u32[]{:S(2)}, u32[]{:S(2)}) async-start(bf16[16,20,1]{1,2,0:T(2,128)(2,1)} %reshape.163), calls=%async_computation.1 | async-start | bytes 16384 | tf_op jit(solution)/shard_map/all_to_all | solution.py:84
  33.6 0.7 broadcast_multiply_fusion
  34.3 0.0 collective-permute-done
  34.3 0.0 collective-permute-done.1
  34.3 0.0 collective-permute-done.2
  34.3 0.0 collective-permute-done.3
  34.3 6.8 %fusion.57 = (bf16[16,16,12,128]{3,2,1,0:T(8,128)(2,1)}, f32[16,16,12,128]{3,2,1,0:T(8,128)}) fusion(f32[16,16]{1,0:T(8,128)S(1)} %broadcast_multiply_fusion, f32[16,16,12,128]{3,2,1,0:T(8,128)} %copy-done.1, f32[16,1,12,128]{3,2,1,0:T(8,128)} %collective-permute-done.3, f32[16,1,12,128]{3,2,1,0:T(8,128)S(1)} %collective-permute-done.2, ...), kind=kLoop, calls=%fused_computation.64 | loop fusion | flops 5898240 | bytes 4332544 | tf_op jit(solution)/shard_map/convert_element_type | solution.py:73
  41.1 0.0 copy-done.4
  41.1 3.6 %scatter_custom_fusion = bf16[321,1536]{1,0:T(8,128)(2,1)} fusion(s32[256]{0:T(256)S(1)} %bitcast.77, bf16[32,8,12,128]{3,2,1,0:T(8,128)(2,1)} %bitcast.73, bf16[]{:T(256)} %constant.7.clone.1), kind=kCustom, calls=%fused_computation.30 | custom fusion | bytes 1772546 | tf_op jit(solution)/shard_map/scatter | solution.py:77
  44.7 2.2 %slice.85 = bf16[320,1536]{1,0:T(8,128)(2,1)} slice(bf16[321,1536]{1,0:T(8,128)(2,1)} %scatter_custom_fusion), slice={[0:320], [0:1536]} | slice | bytes 1966080 | tf_op jit(solution)/shard_map/slice | solution.py:78
  46.9 0.0 copy-start.3
  46.9 2.2 %reshape.127 = bf16[16,20,1536]{2,1,0:T(8,128)(2,1)} reshape(bf16[320,1536]{1,0:T(8,128)(2,1)} %slice.85) | data formatting | bytes 1966080 | tf_op jit(solution)/shard_map/reshape | solution.py:78
  49.1 0.0 copy-start.6
  49.1 0.0 copy-start.7
  49.1 0.0 all-to-all-done.1
  49.1 7.1 %all-to-all-start = ((bf16[16,20,1536]{2,1,0:T(8,128)(2,1)}), bf16[16,20,1536]{2,1,0:T(8,128)(2,1)}, u32[]{:S(2)}, u32[]{:S(2)}) async-start(bf16[16,20,1536]{2,1,0:T(8,128)(2,1)} %reshape.127), calls=%async_computation | async-start | bytes 2359296 | tf_op jit(solution)/shard_map/all_to_all | solution.py:83
  56.2 0.0 copy-done.3
  56.3 0.1 reshape.132
  56.3 26.9 %all-to-all-done = bf16[16,20,1536]{2,1,0:T(8,128)(2,1)} async-done(((bf16[16,20,1536]{2,1,0:T(8,128)(2,1)}), bf16[16,20,1536]{2,1,0:T(8,128)(2,1)}, u32[]{:S(2)}, u32[]{:S(2)}) %all-to-all-start) | async-done | bytes 983072 | tf_op jit(solution)/shard_map/all_to_all | solution.py:83
  83.2 2.1 %reshape.128 = bf16[320,1536]{1,0:T(8,128)(2,1)} reshape(bf16[16,20,1536]{2,1,0:T(8,128)(2,1)} %all-to-all-done) | data formatting | bytes 1966080 | tf_op jit(solution)/shard_map/reshape | solution.py:42
  85.3 0.0 copy-done
  85.3 0.0 copy-done.6
  85.3 0.0 copy-done.7
  85.3 4.9 %multiply_convert_fusion.1 = bf16[320,1024]{1,0:T(8,128)(2,1)} fusion(bf16[1,2,1024,1024]{3,2,1,0:T(8,128)(2,1)} %param.21, bf16[320,1536]{1,0:T(8,128)(2,1)} %reshape.128, bf16[1,1536,1024]{2,1,0:T(8,128)(2,1)S(1)} %copy-done, f32[1024]{0:T(1024)S(1)} %bitcast.81, f32[1024]{0:T(1024)S(1)} %bitcast.83, f32[320]{0:T(512)S(1)} %reshape.132, f32[1024]{0:T(1024)S(1)} %bitcast.84), kind=kOutput, calls=%fused_computation.26 | convolution fusion | flops 1682309120 | bytes 6894848 | tf_op jit(solution)/shard_map/dot_general | solution.py:48
  90.2 0.0 copy-start.5
  90.2 3.3 %convolution_convert_fusion = bf16[320,512]{1,0:T(8,128)(2,1)S(1)} fusion(bf16[1,1024,512]{2,1,0:T(8,128)(2,1)} %param.23, bf16[320,1024]{1,0:T(8,128)(2,1)} %multiply_convert_fusion.1, bf16[1,2,1024,1024]{3,2,1,0:T(8,128)(2,1)} %param.21, f32[1024]{0:T(1024)S(1)} %bitcast.80), kind=kOutput, calls=%fused_computation.28 | convolution fusion | flops 1008762880 | bytes 4132864 | tf_op jit(solution)/shard_map/dot_general | solution.py:52
  93.5 0.8 reshape.130
  94.3 6.2 %all-to-all-start.2 = ((bf16[16,20,512]{2,1,0:T(8,128)(2,1)}), bf16[16,20,512]{2,1,0:T(8,128)(2,1)S(1)}, u32[]{:S(2)}, u32[]{:S(2)}) async-start(bf16[16,20,512]{2,1,0:T(8,128)(2,1)} %reshape.130), calls=%async_computation.2 | async-start | bytes 786432 | tf_op jit(solution)/shard_map/all_to_all | solution.py:92
  100.6 0.0 copy-done.5
  100.6 11.4 %all-to-all-done.2 = bf16[16,20,512]{2,1,0:T(8,128)(2,1)S(1)} async-done(((bf16[16,20,512]{2,1,0:T(8,128)(2,1)}), bf16[16,20,512]{2,1,0:T(8,128)(2,1)S(1)}, u32[]{:S(2)}, u32[]{:S(2)}) %all-to-all-start.2) | async-done | bytes 327712 | tf_op jit(solution)/shard_map/all_to_all | solution.py:92
  112.0 0.8 reshape.131
  112.8 1.0 concatenate.21
  113.8 1.8 %gather_fusion = bf16[256,512]{1,0:T(8,128)(2,1)} fusion(bf16[321,512]{1,0:T(8,128)(2,1)S(1)} %concatenate.21, s32[1024]{0:T(1024)S(1)} %pad_clamp_fusion), kind=kCustom, calls=%fused_computation | custom fusion | bytes 525312 | tf_op jit(solution)/shard_map/gather | solution.py:94
  115.6 1.9 %reshape.133 = f32[16,16,4,128]{3,2,1,0:T(4,128)} reshape(bf16[256,512]{1,0:T(8,128)(2,1)} %gather_fusion) | data formatting | bytes 786432 | tf_op jit(solution)/shard_map/convert_element_type | solution.py:94
  117.5 2.3 %slice_add_fusion = f32[16,16,4,128]{3,2,1,0:T(4,128)} fusion(f32[16,16,4,128]{3,2,1,0:T(4,128)} %reshape.133, f32[16,16,12,128]{3,2,1,0:T(8,128)} %get-tuple-element.6), kind=kLoop, calls=%fused_computation.39 | loop fusion | flops 131072 | bytes 1572864 | tf_op jit(solution)/shard_map/add | solution.py:95
  (4 shorter events, 0.1 us)
Async XLA Ops:
  0.0 85.3 %copy-start = (bf16[1,1536,1024]{2,1,0:T(8,128)(2,1)S(1)}, bf16[1,1536,1024]{2,1,0:T(8,128)(2,1)}, u32[]{:S(2)}) copy-start(bf16[1,1536,1024]{2,1,0:T(8,128)(2,1)} %param.18) | copy-start | bytes 9437188
  0.0 14.3 %copy-start.2 = (s32[1,1,1,256,1]{3,4,2,1,0:T(1,128)S(1)}, s32[1,1,1,256,1]{3,4,2,1,0:T(1,128)}, u32[]{:S(2)}) copy-start(s32[1,1,1,256,1]{3,4,2,1,0:T(1,128)} %param.16) | copy-start | bytes 3076
  2.1 5.9 %copy-start.1 = (f32[16,16,12,128]{3,2,1,0:T(8,128)}, f32[16,16,12,128]{3,2,1,0:T(8,128)S(1)}, u32[]{:S(2)}) copy-start(f32[16,16,12,128]{3,2,1,0:T(8,128)S(1)} %copy.43) | copy-start | bytes 4718596
  2.9 31.4 %collective-permute-start = (f32[1,16,12,128]{3,2,1,0:T(8,128)}, f32[1,16,12,128]{3,2,1,0:T(8,128)S(1)}, u32[]{:S(2)}, u32[]{:S(2)}) collective-permute-start(f32[1,16,12,128]{3,2,1,0:T(8,128)} %get-tuple-element.7), channel_id=1, source_target_pairs={{8,0},{16,8},{24,16},{0,24},{9,1},{17,9},{25,17},{1,25},{10,2},{18... | collective-permute-start | bytes 294920 | tf_op jit(solution)/shard_map/ppermute | solution.py:17
  7.9 26.3 %collective-permute-start.1 = (f32[1,16,12,128]{3,2,1,0:T(8,128)}, f32[1,16,12,128]{3,2,1,0:T(8,128)S(1)}, u32[]{:S(2)}, u32[]{:S(2)}) collective-permute-start(f32[1,16,12,128]{3,2,1,0:T(8,128)} %get-tuple-element.8), channel_id=1, source_target_pairs={{0,8},{8,16},{16,24},{24,0},{1,9},{9,17},{17,25},{25,1},{2,10},{10... | collective-permute-start | bytes 294920 | tf_op jit(solution)/shard_map/ppermute | solution.py:14
  8.7 25.6 %collective-permute-start.2 = (f32[16,1,12,128]{3,2,1,0:T(8,128)}, f32[16,1,12,128]{3,2,1,0:T(8,128)S(1)}, u32[]{:S(2)}, u32[]{:S(2)}) collective-permute-start(f32[16,1,12,128]{3,2,1,0:T(8,128)} %get-tuple-element.9), channel_id=1, source_target_pairs={{1,0},{2,1},{3,2},{4,3},{5,4},{6,5},{7,6},{9,8},{10,9},{11,10},{12... | collective-permute-start | bytes 294920 | tf_op jit(solution)/shard_map/ppermute | solution.py:17
  9.9 24.3 %collective-permute-start.3 = (f32[16,1,12,128]{3,2,1,0:T(8,128)}, f32[16,1,12,128]{3,2,1,0:T(8,128)}, u32[]{:S(2)}, u32[]{:S(2)}) collective-permute-start(f32[16,1,12,128]{3,2,1,0:T(8,128)} %get-tuple-element.10), channel_id=1, source_target_pairs={{0,1},{1,2},{2,3},{3,4},{4,5},{5,6},{6,7},{8,9},{9,10},{10,11},{11... | collective-permute-start | bytes 294920 | tf_op jit(solution)/shard_map/ppermute | solution.py:14
  24.1 17.0 %copy-start.4 = (s32[256,1]{0,1:T(1,128)}, s32[256,1]{0,1:T(1,128)S(1)}, u32[]{:S(2)}) copy-start(s32[256,1]{0,1:T(1,128)S(1)} %compare_select_fusion) | copy-start | bytes 3076
  27.1 22.0 %all-to-all-start.1 = ((bf16[16,20,1]{1,2,0:T(2,128)(2,1)}), bf16[16,20,1]{1,2,0:T(2,128)(2,1)S(1)}, u32[]{:S(2)}, u32[]{:S(2)}) async-start(bf16[16,20,1]{1,2,0:T(2,128)(2,1)} %reshape.163), calls=%async_computation.1 | async-start | bytes 16384 | tf_op jit(solution)/shard_map/all_to_all | solution.py:84
  46.9 9.3 %copy-start.3 = (f32[1,2,1024]{2,1,0:T(2,128)S(1)}, f32[1,2,1024]{2,1,0:T(2,128)}, u32[]{:S(2)}) copy-start(f32[1,2,1024]{2,1,0:T(2,128)} %param.22) | copy-start | bytes 24580
  49.1 36.3 %copy-start.6 = (f32[1,1024]{1,0:T(1,128)S(1)}, f32[1,1024]{1,0:T(1,128)}, u32[]{:S(2)}) copy-start(f32[1,1024]{1,0:T(1,128)} %param.20) | copy-start | bytes 12292
  49.1 36.3 %copy-start.7 = (f32[1,1024]{1,0:T(1,128)S(1)}, f32[1,1024]{1,0:T(1,128)}, u32[]{:S(2)}) copy-start(f32[1,1024]{1,0:T(1,128)} %param.19) | copy-start | bytes 12292
  49.1 34.1 %all-to-all-start = ((bf16[16,20,1536]{2,1,0:T(8,128)(2,1)}), bf16[16,20,1536]{2,1,0:T(8,128)(2,1)}, u32[]{:S(2)}, u32[]{:S(2)}) async-start(bf16[16,20,1536]{2,1,0:T(8,128)(2,1)} %reshape.127), calls=%async_computation | async-start | bytes 2359296 | tf_op jit(solution)/shard_map/all_to_all | solution.py:83
  90.2 10.3 %copy-start.5 = (s32[256,1]{0,1:T(1,128)S(1)}, s32[256,1]{0,1:T(1,128)}, u32[]{:S(2)}) copy-start(s32[256,1]{0,1:T(1,128)} %copy-done.4) | copy-start | bytes 3076
  94.3 17.6 %all-to-all-start.2 = ((bf16[16,20,512]{2,1,0:T(8,128)(2,1)}), bf16[16,20,512]{2,1,0:T(8,128)(2,1)S(1)}, u32[]{:S(2)}, u32[]{:S(2)}) async-start(bf16[16,20,512]{2,1,0:T(8,128)(2,1)} %reshape.130), calls=%async_computation.2 | async-start | bytes 786432 | tf_op jit(solution)/shard_map/all_to_all | solution.py:92
where the time goes:
time: 121 us; the launch traced here: 120 us
  waiting for transfers between devices  38.3 us (32%)
  starting transfers between devices  29.8 us (25%)
  local copies, waits for them, and re-layouts  26.4 us (22%)
  other arithmetic  16.4 us (14%)
  matrix products  8.18 us (7%)
    all_to_all x1, waiting for transfers between devices, body(): lax.all_to_all(outbound, ('tile', 'lat'), split_axis=0, concat_axis=0, ti...  26.9 us
    all_to_all x1, waiting for transfers between devices, body(): lax.all_to_all(produced, ('tile', 'lat'), split_axis=0, concat_axis=0, ti...  11.4 us
    all_to_all x1, starting transfers between devices, body(): lax.all_to_all(outbound, ('tile', 'lat'), split_axis=0, concat_axis=0, ti...  7.09 us
    convert_element_type x1, other arithmetic, body(): features = advanced.astype(jnp.bfloat16).reshape(columns, fsize)  6.83 us
    all_to_all x1, starting transfers between devices, body(): lax.all_to_all(flags, ('tile', 'lat'), split_axis=0, concat_axis=0, tiled...  6.45 us
    ppermute x2, starting transfers between devices, extended(): lax.ppermute(lax.slice_in_dim(block, 0, width, axis=dim), axis, backward)  6.36 us
    all_to_all x1, starting transfers between devices, body(): lax.all_to_all(produced, ('tile', 'lat'), split_axis=0, concat_axis=0, ti...  6.23 us
    dot_general x1, matrix products, run_network(): jnp.dot(hidden, w_inner[number], preferred_element_type=jnp.float32)  4.9 us
  transfers between devices with their start and end apart: 7, of which 2 were waited for; matrix products, arithmetic and copies ran while one was open for 24% of the time, Pallas kernels for 0%

commit v1 on v0

v1 whole, which is shorter than its diff:
```python
import functools
import math

import jax
import jax.numpy as jnp
from jax import lax
from jax.experimental import pallas as pl
from jax.experimental.pallas import tpu as pltpu
from jax.sharding import PartitionSpec as P

F32 = jnp.float32
BF16 = jnp.bfloat16
VM = pl.BlockSpec(memory_space=pltpu.VMEM)
SM = pl.BlockSpec(memory_space=pltpu.SMEM)


class Plan:
    def __init__(self, experts, capacity):
        self.experts = experts
        self.full = capacity // 16 * 16
        self.rest = capacity - self.full
        self.group = 8 // math.gcd(self.rest, 8) if self.rest else 1
        self.chunk = self.group * self.rest

    def rows(self, variables):
        return variables * (self.full + self.rest)

    def spot(self, number, variables):
        return (number % self.group) * (variables // self.group) + number // self.group


def iota(shape, dim):
    return lax.broadcasted_iota(jnp.int32, shape, dim)


def hot(match):
    return jnp.where(match, 1.0, 0.0).astype(BF16)


def spread(plan, place):
    small, large = plan.experts * plan.rest, plan.experts * plan.chunk
    row = iota((small, large), 0)
    if plan.rest & (plan.rest - 1) == 0:
        source = lax.shift_right_logical(row, plan.rest.bit_length() - 1)
    else:
        source = lax.div(row, plan.rest)
    return row + source * (plan.chunk - plan.rest) + place * plan.rest, iota((small, large), 1)


def route_kernel(plan, count_ref, routes_ref, land_ref, wind_ref, *refs):
    refs = list(refs)
    flags_ref, wind_out = refs[:2]
    refs = refs[2:]
    column_ref = refs.pop()
    experts = plan.experts
    columns = routes_ref.shape[1]
    lons, lats = land_ref.shape
    routes = routes_ref[...]
    active = iota((1, columns), 1) < count_ref[0, 0]
    owner = (iota((experts, columns), 0) == routes) & active
    owner_hot = hot(owner)
    earlier = hot(iota((columns, columns), 0) < iota((columns, columns), 1))
    before = jnp.dot(owner_hot, earlier, preferred_element_type=F32)
    rank = jnp.sum(jnp.where(owner, before, 0.0), axis=0, keepdims=True)
    diagonal = iota((columns, columns), 0) == iota((columns, columns), 1)

    def upright(row):
        return jnp.sum(jnp.where(diagonal, row, 0.0), axis=1, keepdims=True)

    rank_int = rank.astype(jnp.int32)
    if plan.full:
        target = jnp.where(active & (rank_int < plan.full), routes * plan.full + rank_int, -1)
        total = experts * plan.full
        refs.pop(0)[...] = hot(iota((total, columns), 0) == target)
        tall = upright(target.astype(F32)).astype(jnp.int32)
        refs.pop(0)[...] = hot(iota((columns, total), 1) == tall)
    if plan.rest:
        pack_ref, pick_ref = refs.pop(0), refs.pop(0)
        total = experts * plan.chunk
        held = active & (rank_int >= plan.full)
        base = routes * plan.chunk + rank_int - plan.full
        for place in range(plan.group):
            target = jnp.where(held, base + place * plan.rest, -1)
            pack_ref[:, place * columns : (place + 1) * columns] = hot(
                iota((total, columns), 0) == target
            )
            tall = upright(target.astype(F32)).astype(jnp.int32)
            pick_ref[:, place * total : (place + 1) * total] = hot(
                iota((columns, total), 1) == tall
            )
    eye = iota((lats, lats), 0) == iota((lats, lats), 1)
    for lon in range(lons):
        rows = slice(lon * lats, (lon + 1) * lats)
        flag = jnp.where(eye, land_ref[lon : lon + 1, :].astype(F32), 0.0)
        column_ref[rows, :] = jnp.broadcast_to(
            jnp.sum(flag, axis=1, keepdims=True), (lats, column_ref.shape[1])
        )
        half = jnp.where(eye, 0.5 * wind_ref[lon : lon + 1, :], 0.0)
        wind_out[rows, :] = jnp.broadcast_to(
            jnp.sum(half, axis=1, keepdims=True), (lats, wind_out.shape[1])
        )
    lanes = flags_ref.shape[1]
    at = upright(rank).astype(jnp.int32) == iota((columns, lanes), 1)
    marked = jnp.where(at, column_ref[...], 0.0).astype(BF16)
    flags_ref[...] = jnp.dot(owner_hot, marked, preferred_element_type=F32)


def stencil_kernel(
    plan, state_ref, west_ref, east_ref, south_ref, north_ref, diff_ref, wind_ref, flags_ref, *refs
):
    refs = list(refs)
    pack_full = refs.pop(0) if plan.full else None
    pack_rest = refs.pop(0) if plan.rest else None
    out_ref, kept_ref, feature_ref = refs
    lons, variables, lats, levels = state_ref.shape
    columns = lons * lats
    kept = kept_ref.shape[1]
    row = iota((lats, levels), 0)
    for number in range(variables):
        spread_by = diff_ref[number : number + 1, :]
        spot = plan.spot(number, variables)
        for lon in range(lons):
            center = state_ref[lon, number]
            east = state_ref[lon + 1, number] if lon + 1 < lons else east_ref[number]
            west = state_ref[lon - 1, number] if lon else west_ref[number]
            north = jnp.where(
                row == lats - 1,
                north_ref[lon, number : number + 1, :],
                pltpu.roll(center, lats - 1, 0),
            )
            south = jnp.where(
                row == 0, south_ref[lon, number : number + 1, :], pltpu.roll(center, 1, 0)
            )
            total = east + west + north + south - 4.0 * center
            half = wind_ref[lon * lats : (lon + 1) * lats, :]
            moved = center + spread_by * total - half * (east - west)
            if number < kept:
                kept_ref[lon, number] = moved
            feature_ref[lon * lats : (lon + 1) * lats, spot * levels : (spot + 1) * levels] = (
                moved.astype(BF16)
            )
    experts = plan.experts
    if plan.full:
        packed = jnp.dot(pack_full[...], feature_ref[...], preferred_element_type=F32)
        for number in range(variables):
            spot = plan.spot(number, variables)
            block = packed[:, spot * levels : (spot + 1) * levels].astype(BF16)
            out_ref[:, number * plan.full : (number + 1) * plan.full, :] = block.reshape(
                experts, plan.full, levels
            )
    start = variables * plan.full
    if plan.rest:
        groups = variables // plan.group
        packed = jnp.zeros((experts * plan.chunk, groups * levels), F32)
        for place in range(plan.group):
            packed += jnp.dot(
                pack_rest[:, place * columns : (place + 1) * columns],
                feature_ref[:, place * groups * levels : (place + 1) * groups * levels],
                preferred_element_type=F32,
            )
        for group in range(groups):
            block = packed[:, group * levels : (group + 1) * levels]
            out_ref[:, start : start + plan.chunk, :] = block.reshape(
                experts, plan.chunk, levels
            ).astype(BF16)
            start += plan.chunk
    out_ref[:, start : start + 8, :] = jnp.broadcast_to(
        flags_ref[...].reshape(experts, 1, levels), (experts, 8, levels)
    ).astype(BF16)


def network_kernel(
    plan, rows_ref, w_first, b_first, land_add, w_inner, b_inner, w_last, out_ref, x_ref
):
    sources, _, levels = rows_ref.shape
    variables = w_first.shape[0] // levels
    lead = sources * plan.full
    small = sources * plan.rest
    marks = rows_ref[:, plan.rows(variables) :, :].astype(F32)
    flags = []
    if plan.full:
        for number in range(variables):
            block = rows_ref[:, number * plan.full : (number + 1) * plan.full, :]
            x_ref[:lead, number * levels : (number + 1) * levels] = block.reshape(lead, levels)
        tall = jnp.concatenate([marks] * (plan.full // 8), axis=1)
        match = iota(tall.shape, 1) == iota(tall.shape, 2)
        flags.append(jnp.sum(jnp.where(match, tall, 0.0), axis=2, keepdims=True).reshape(lead, 1))
    if plan.rest:
        start = variables * plan.full
        groups = variables // plan.group
        blocks = []
        for group in range(groups):
            block = rows_ref[:, start : start + plan.chunk, :].astype(F32)
            blocks.append(block.reshape(sources * plan.chunk, levels).astype(BF16))
            start += plan.chunk
        mixed = jnp.concatenate(blocks, axis=1)
        for place in range(plan.group):
            target, column = spread(plan, place)
            picked = jnp.dot(hot(target == column), mixed, preferred_element_type=F32)
            for group in range(groups):
                number = group * plan.group + place
                x_ref[lead:, number * levels : (number + 1) * levels] = picked[
                    :, group * levels : (group + 1) * levels
                ].astype(BF16)
        tall = jnp.concatenate([marks] * (plan.chunk // 8), axis=1)
        match = iota(tall.shape, 2) == iota(tall.shape, 1) + plan.full
        tall = jnp.sum(jnp.where(match, tall, 0.0), axis=2, keepdims=True)
        tall = jnp.broadcast_to(tall, (sources, plan.chunk, levels))
        tall = tall.reshape(sources * plan.chunk, levels).astype(BF16)
        target, column = spread(plan, 0)
        flags.append(jnp.dot(hot(target == column), tall, preferred_element_type=F32)[:, :1])
    flag = jnp.concatenate(flags, axis=0)
    pre = jnp.dot(x_ref[...], w_first[...], preferred_element_type=F32) + b_first[...]
    hidden = jax.nn.silu(pre + flag * land_add[...]).astype(BF16)
    for number in range(w_inner.shape[0]):
        pre = jnp.dot(hidden, w_inner[number], preferred_element_type=F32)
        hidden = jax.nn.silu(pre + b_inner[number : number + 1, :]).astype(BF16)
    made = jnp.dot(hidden, w_last[...], preferred_element_type=F32).astype(BF16)
    outs = made.shape[1] // levels
    if plan.full:
        for number in range(outs):
            block = made[:lead, number * levels : (number + 1) * levels]
            out_ref[:, number * plan.full : (number + 1) * plan.full, :] = block.reshape(
                sources, plan.full, levels
            )
    if plan.rest:
        start = outs * plan.full
        groups = outs // plan.group
        packed = jnp.zeros((sources * plan.chunk, groups * levels), F32)
        for place in range(plan.group):
            parts = [
                made[lead:, number * levels : (number + 1) * levels]
                for number in range(place, outs, plan.group)
            ]
            part = jnp.concatenate(parts, axis=1)
            target, column = spread(plan, place)
            packed += lax.dot_general(
                hot(target == column), part, (((0,), (0,)), ((), ())), preferred_element_type=F32
            )
        for group in range(groups):
            block = packed[:, group * levels : (group + 1) * levels]
            out_ref[:, start : start + plan.chunk, :] = block.reshape(
                sources, plan.chunk, levels
            ).astype(BF16)
            start += plan.chunk


def finish_kernel(plan, rows_ref, kept_ref, *refs):
    refs = list(refs)
    pick_full = refs.pop(0) if plan.full else None
    pick_rest = refs.pop(0) if plan.rest else None
    (out_ref,) = refs
    experts, _, levels = rows_ref.shape
    lons, outs, lats, _ = kept_ref.shape
    columns = lons * lats
    found = [None] * outs
    if plan.full:
        blocks = [
            rows_ref[:, number * plan.full : (number + 1) * plan.full, :].reshape(
                experts * plan.full, levels
            )
            for number in range(outs)
        ]
        full = jnp.dot(
            pick_full[...], jnp.concatenate(blocks, axis=1), preferred_element_type=F32
        )
        found = [full[:, number * levels : (number + 1) * levels] for number in range(outs)]
    if plan.rest:
        start = outs * plan.full
        groups = outs // plan.group
        total = experts * plan.chunk
        blocks = []
        for group in range(groups):
            block = rows_ref[:, start : start + plan.chunk, :].astype(F32)
            blocks.append(block.reshape(total, levels).astype(BF16))
            start += plan.chunk
        mixed = jnp.concatenate(blocks, axis=1)
        for place in range(plan.group):
            part = jnp.dot(
                pick_rest[:, place * total : (place + 1) * total],
                mixed,
                preferred_element_type=F32,
            )
            for group in range(groups):
                number = group * plan.group + place
                piece = part[:, group * levels : (group + 1) * levels]
                found[number] = piece if found[number] is None else found[number] + piece
    for number in range(outs):
        base = kept_ref[:, number].reshape(columns, levels)
        out_ref[pl.ds(number, columns, stride=outs), :] = base + found[number]


def call(kernel, specs, shapes, scratch=()):
    return pl.pallas_call(
        kernel,
        in_specs=specs,
        out_specs=jax.tree.map(lambda _: VM, shapes),
        out_shape=shapes,
        scratch_shapes=list(scratch),
        compiler_params=pltpu.CompilerParams(vmem_limit_bytes=48 * 1024 * 1024),
    )


def shape(dims, dtype):
    return jax.ShapeDtypeStruct(tuple(dims), dtype)


def exchanged(state):
    tiles = lax.axis_size("tile")
    bands = lax.axis_size("lat") * lax.axis_size("emu")
    up = [(i, (i + 1) % tiles) for i in range(tiles)]
    west = lax.ppermute(state[-1], "tile", up)
    east = lax.ppermute(state[0], "tile", [(b, a) for a, b in up])
    along = [(i, i + 1) for i in range(bands - 1)]
    south = lax.ppermute(state[:, :, -1, :], ("lat", "emu"), along)
    north = lax.ppermute(state[:, :, 0, :], ("lat", "emu"), [(b, a) for a, b in along])
    return west, east, south, north


def body(
    state, diffusivity, wind, land_mask, routes, counts, w_in, b_in, land_vec, w_hid, b_hid, w_out
):
    lons, lats, variables, levels = state.shape
    columns = lons * lats
    outs = w_out.shape[2] // levels
    experts = lax.axis_size("tile") * lax.axis_size("lat")
    capacity = max(2, columns * 5 // (4 * experts))
    plan = Plan(experts, capacity)
    state = jnp.transpose(state, (0, 2, 1, 3))
    halos = exchanged(state)

    shapes = [shape((experts, levels), F32), shape((columns, levels), F32)]
    if plan.full:
        total = experts * plan.full
        shapes += [shape((total, columns), BF16), shape((columns, total), BF16)]
    if plan.rest:
        total = experts * plan.chunk
        shapes += [
            shape((total, plan.group * columns), BF16),
            shape((columns, plan.group * total), BF16),
        ]
    made = call(
        functools.partial(route_kernel, plan),
        [SM, VM, VM, VM],
        shapes,
        [pltpu.VMEM((columns, levels), F32)],
    )(counts.reshape(1, 1), routes.reshape(1, columns), land_mask, wind)
    flags, half_wind = made[:2]
    packs, picks = made[2::2], made[3::2]

    rows, kept = call(
        functools.partial(stencil_kernel, plan),
        [VM] * (8 + len(packs)),
        [
            shape((experts, plan.rows(variables) + 8, levels), BF16),
            shape((lons, outs, lats, levels), F32),
        ],
        [pltpu.VMEM((columns, variables * levels), BF16)],
    )(state, *halos, diffusivity, half_wind, flags, *packs)

    axes = ("tile", "lat")
    rows = lax.all_to_all(rows, axes, split_axis=0, concat_axis=0, tiled=True)
    made = call(
        functools.partial(network_kernel, plan),
        [VM] * 7,
        shape((experts, plan.rows(outs), levels), BF16),
        [pltpu.VMEM((experts * capacity, variables * levels), BF16)],
    )(rows, w_in[0], b_in, land_vec, w_hid[0], b_hid[0], w_out[0])
    made = lax.all_to_all(made, axes, split_axis=0, concat_axis=0, tiled=True)
    out = call(
        functools.partial(finish_kernel, plan),
        [VM] * (2 + len(picks)),
        shape((columns * outs, levels), F32),
    )(made, kept, *picks)
    return out.reshape(lons, lats, outs, levels)


def solution(mesh):
    in_specs = (
        P("tile", ("lat", "emu"), None, None),
        P(),
        P("tile", ("lat", "emu")),
        P("tile", ("lat", "emu")),
        P("tile", "lat", "emu", None, None),
        P("tile", "lat", "emu"),
        P(("tile", "lat"), None, None),
        P(("tile", "lat"), None),
        P(("tile", "lat"), None),
        P(("tile", "lat"), None, None, None),
        P(("tile", "lat"), None, None),
        P(("tile", "lat"), None, None),
    )
    out_specs = P("tile", ("lat", "emu"), None, None)
    return jax.shard_map(body, mesh=mesh, in_specs=in_specs, out_specs=out_specs, check_vma=False)
```

time: 121 us -> 70.7 us (0.58)
  blocking collectives: 0 us -> 48.8 us
  waiting for transfers between devices: 38.3 us -> 2.44 us
  local copies, waits for them, and re-layouts: 26.4 us -> 2.22 us
  starting transfers between devices: 29.8 us -> 7.97 us
  other arithmetic: 16.4 us -> 0 us
  Pallas kernels: 0 us -> 8.28 us
  matrix products: 8.18 us -> 0 us
    all_to_all x0 -> x2, blocking collectives: none -> 48.8 us  [the longest x1 32.5 us: body(): rows = lax.all_to_all(rows, axes, split_axis=0, concat_axis=0, tiled=True)]
    all_to_all x3 -> x0, waiting for transfers between devices: 38.2 us -> none  [the longest x1 26.9 us: body(): lax.all_to_all(outbound, ('tile', 'lat'), split_axis=0, concat_axis=0, ti...]
    all_to_all x3 -> x0, starting transfers between devices: 19.8 us -> none  [the longest x1 7.09 us: body(): lax.all_to_all(outbound, ('tile', 'lat'), split_axis=0, concat_axis=0, ti...]
    convert_element_type x4 -> x0, other arithmetic: 8.75 us -> none  [the longest x1 6.83 us: body(): features = advanced.astype(jnp.bfloat16).reshape(columns, fsize)]
    pallas_call x0 -> x4, Pallas kernels: none -> 8.28 us  [the longest x1 5.38 us: body(): call(functools.partial(network_kernel, plan), [VM] * 7, shape((experts, p...]
    dot_general x2 -> x0, matrix products: 8.18 us -> none  [the longest x1 4.9 us: run_network(): jnp.dot(hidden, w_inner[number], preferred_element_type=jnp.float32)]
    reshape x5 -> x0, local copies, waits for them, and re-layouts: 6.59 us -> none  [the longest x1 2.16 us: body(): outbound = outbound[:-1].reshape(experts, capacity, fsize)]
    scatter x2 -> x0, local copies, waits for them, and re-layouts: 5.86 us -> none  [the longest x1 3.57 us: body(): jnp.zeros((experts * capacity + 1, fsize), jnp.bfloat16).at[slot_index]]
  transfers between devices with their start and end apart: 7 -> 4, of which waited for: 2 -> 3; matrix products, arithmetic and copies ran while one was open for 24% -> 0% of each run, Pallas kernels for 0% -> 1%
where the time goes in v1:
time: 70.7 us; the launch traced here: 70.5 us
  blocking collectives  48.8 us (69%)
  Pallas kernels  8.28 us (12%)
  starting transfers between devices  7.97 us (11%)
  waiting for transfers between devices  2.44 us (3%)
  local copies, waits for them, and re-layouts  2.22 us (3%)
  between operations  0.8 us (1%)
    all_to_all x1, blocking collectives, body(): rows = lax.all_to_all(rows, axes, split_axis=0, concat_axis=0, tiled=True)  32.5 us
    all_to_all x1, blocking collectives, body(): made = lax.all_to_all(made, axes, split_axis=0, concat_axis=0, tiled=True)  16.3 us
    pallas_call x1, Pallas kernels, body(): call(functools.partial(network_kernel, plan), [VM] * 7, shape((experts, p...  5.38 us
    ppermute x1, starting transfers between devices, exchanged(): west = lax.ppermute(state[-1], 'tile', up)  3.12 us
    unnamed x21, local copies, waits for them, and re-layouts  2.11 us
    ppermute x1, starting transfers between devices, exchanged(): east = lax.ppermute(state[0], 'tile', [(b, a) for a, b in up])  2.09 us
    ppermute x1, starting transfers between devices, exchanged(): south = lax.ppermute(state[:, :, -1, :], ('lat', 'emu'), along)  1.47 us
  transfers between devices with their start and end apart: 4, of which 3 were waited for; matrix products, arithmetic and copies ran while one was open for 0% of the time, Pallas kernels for 1%

profile of v1, /device:TPU:0, one launch (start us, length us, event | category | flops | bytes accessed | tf_op | source)
XLA Modules:
  0.0 70.5 jit_solution(13885074265477025456)
XLA Ops:
  0.0 0.0 copy-start
  0.0 0.0 copy-start.9
  0.0 0.0 copy-start.5
  0.0 0.0 copy-start.6
  0.0 0.0 copy-start.3
  0.0 2.1 %copy.19 = f32[16,16,12,128]{3,2,0,1:T(8,128)S(1)} copy(f32[16,16,12,128]{3,1,2,0:T(8,128)} %param.12) | data formatting | bytes 3145728 | tf_op args[0]
  2.1 3.1 %collective-permute-start = (f32[12,16,128]{2,0,1:T(8,128)S(1)}, f32[12,16,128]{2,0,1:T(8,128)S(1)}, u32[]{:S(2)}, u32[]{:S(2)}) collective-permute-start(f32[12,16,128]{2,0,1:T(8,128)S(1)} %get-tuple-element.24), channel_id=1, source_target_pairs={{0,8},{8,16},{16,24},{24,0},{1,9},{9,17},{17,25},{25,1},{2,10},{10... | collective-permute-start | bytes 294920 | tf_op jit(solution)/shard_map/ppermute | solution.py:312
  5.2 2.1 %collective-permute-start.1 = (f32[12,16,128]{2,0,1:T(8,128)S(1)}, f32[12,16,128]{2,0,1:T(8,128)S(1)}, u32[]{:S(2)}, u32[]{:S(2)}) collective-permute-start(f32[12,16,128]{2,0,1:T(8,128)S(1)} %get-tuple-element.23), channel_id=1, source_target_pairs={{8,0},{16,8},{24,16},{0,24},{9,1},{17,9},{25,17},{1,25},{10,2},{18... | collective-permute-start | bytes 294920 | tf_op jit(solution)/shard_map/ppermute | solution.py:313
  7.3 1.5 %collective-permute-start.2 = (f32[16,12,128]{2,1,0:T(8,128)S(1)}, f32[16,12,128]{2,1,0:T(8,128)S(1)}, u32[]{:S(2)}, u32[]{:S(2)}) collective-permute-start(f32[16,12,128]{2,1,0:T(8,128)S(1)} %get-tuple-element.22), channel_id=1, source_target_pairs={{0,1},{1,2},{2,3},{3,4},{4,5},{5,6},{6,7},{8,9},{9,10},{10,11},{11... | collective-permute-start | bytes 294920 | tf_op jit(solution)/shard_map/ppermute | solution.py:315
  8.8 1.3 %collective-permute-start.3 = (f32[16,12,128]{2,1,0:T(8,128)S(1)}, f32[16,12,128]{2,1,0:T(8,128)S(1)}, u32[]{:S(2)}, u32[]{:S(2)}) collective-permute-start(f32[16,12,128]{2,1,0:T(8,128)S(1)} %get-tuple-element.21), channel_id=1, source_target_pairs={{1,0},{2,1},{3,2},{4,3},{5,4},{6,5},{7,6},{9,8},{10,9},{11,10},{12... | collective-permute-start | bytes 294920 | tf_op jit(solution)/shard_map/ppermute | solution.py:316
  10.8 0.0 copy-done.9
  10.8 0.0 copy-done.5
  10.8 0.0 copy-done.6
  10.8 0.4 shard_map.118
  11.2 0.4 collective-permute-done
  11.6 1.4 %collective-permute-done.1 = f32[12,16,128]{2,0,1:T(8,128)S(1)} collective-permute-done((f32[12,16,128]{2,0,1:T(8,128)S(1)}, f32[12,16,128]{2,0,1:T(8,128)S(1)}, u32[]{:S(2)}, u32[]{:S(2)}) %collective-permute-start.1) | collective-permute-done | bytes 98336 | tf_op jit(solution)/shard_map/ppermute | solution.py:313
  13.0 0.0 collective-permute-done.2.south_ref
  13.0 0.7 %collective-permute-done.3.north_ref = f32[16,12,128]{2,1,0:T(8,128)S(1)} collective-permute-done((f32[16,12,128]{2,1,0:T(8,128)S(1)}, f32[16,12,128]{2,1,0:T(8,128)S(1)}, u32[]{:S(2)}, u32[]{:S(2)}) %collective-permute-start.3) | collective-permute-done | bytes 98336 | tf_op jit(solution)/shard_map/ppermute | solution.py:316
  13.8 0.0 copy-done
  13.8 0.0 copy-done.3
  13.8 0.0 copy-start.1
  13.8 0.0 copy-start.2
  13.8 0.0 copy-start.4
  13.8 0.0 copy-start.7
  13.8 0.0 copy-start.8
  13.8 1.4 %shard_map.119 = (bf16[16,248,128]{2,1,0:T(8,128)(2,1)S(1)}, f32[16,4,16,128]{3,2,1,0:T(8,128)S(1)}) custom-call(f32[16,12,16,128]{3,2,1,0:T(8,128)S(1)} %bitcast.20, f32[12,16,128]{2,1,0:T(8,128)S(1)} %copy.15.west_ref, f32[12,16,128]{2,1,0:T(8,128)S(1)} %copy.16.east_ref, f32[16,12,128]{2,1,0:T(8,128)S(1)} %collective-permute-done.2.south_ref, ...), custom_call_target="tpu_custom_call" | custom-call | tf_op jit(solution)/shard_map/pallas_call | solution.py:351
  15.2 32.5 %all_to_all.10.rows_ref = bf16[16,248,128]{2,1,0:T(8,128)(2,1)S(1)} all-to-all(bf16[16,248,128]{2,1,0:T(8,128)(2,1)S(1)} %get-tuple-element.17), channel_id=1, replica_groups=mesh['tile'=4,'lat'=4,'emu'=2] {'tile','lat'}, dimensions={0} | all-to-all | bytes 2031616 | tf_op jit(solution)/shard_map/all_to_all | solution.py:362
  47.7 0.0 copy-done.1
  47.7 0.0 copy-done.2
  47.7 0.0 copy-done.4
  47.7 0.0 copy-done.7
  47.7 0.0 copy-done.8
  47.7 5.4 %shard_map.120 = bf16[16,80,128]{2,1,0:T(8,128)(2,1)S(1)} custom-call(bf16[16,248,128]{2,1,0:T(8,128)(2,1)S(1)} %all_to_all.10.rows_ref, bf16[1536,1024]{1,0:T(8,128)(2,1)S(1)} %bitcast.21, f32[1,1024]{1,0:T(1,128)S(1)} %copy-done.7, f32[1,1024]{1,0:T(1,128)S(1)} %copy-done.8, bf16[2,1024,1024]{2,1,0:T(8,128)(2,1)} %bitcast.25, f32[2,1024]{1,0:T(2,128)S(1)} %bitcast.23, ...), custom_call_target="tpu_custom_call" | custom-call | tf_op jit(solution)/shard_map/pallas_call | solution.py:363
  53.1 16.3 %all_to_all.11.rows_ref = bf16[16,80,128]{2,1,0:T(8,128)(2,1)S(1)} all-to-all(bf16[16,80,128]{2,1,0:T(8,128)(2,1)S(1)} %shard_map.120), channel_id=1, replica_groups=mesh['tile'=4,'lat'=4,'emu'=2] {'tile','lat'}, dimensions={0} | all-to-all | bytes 655360 | tf_op jit(solution)/shard_map/all_to_all | solution.py:369
  69.4 1.1 %shard_map.121 = f32[1024,128]{1,0:T(8,128)} custom-call(bf16[16,80,128]{2,1,0:T(8,128)(2,1)S(1)} %all_to_all.11.rows_ref, f32[16,4,16,128]{3,2,1,0:T(8,128)S(1)} %get-tuple-element.18.kept_ref, bf16[256,256]{1,0:T(8,128)(2,1)S(1)} %get-tuple-element.19.refs_0_, bf16[256,256]{1,0:T(8,128)(2,1)S(1)} %get-tuple-element.20.refs_1_), custom_call_target="tpu_custom_call" | custom-call | tf_op jit(solution)/shard_map/pallas_call | solution.py:370
  (4 shorter events, 0.1 us)
Async XLA Ops:
  0.0 13.8 %copy-start = (f32[16,16,12,128]{3,1,2,0:T(8,128)S(1)}, f32[16,16,12,128]{3,1,2,0:T(8,128)}, u32[]{:S(2)}) copy-start(f32[16,16,12,128]{3,1,2,0:T(8,128)} %param.12) | copy-start | bytes 4718596
  0.0 10.8 %copy-start.9 = (s32[1,1,1,256,1]{3,4,2,1,0:T(1,128)S(1)}, s32[1,1,1,256,1]{3,4,2,1,0:T(1,128)}, u32[]{:S(2)}) copy-start(s32[1,1,1,256,1]{3,4,2,1,0:T(1,128)} %param.16) | copy-start | bytes 3076
  0.0 10.8 %copy-start.5 = (s32[16,16]{1,0:T(8,128)S(1)}, s32[16,16]{1,0:T(8,128)}, u32[]{:S(2)}) copy-start(s32[16,16]{1,0:T(8,128)} %land_ref.1) | copy-start | bytes 3076
  0.0 10.8 %copy-start.6 = (f32[16,16]{1,0:T(8,128)S(1)}, f32[16,16]{1,0:T(8,128)}, u32[]{:S(2)}) copy-start(f32[16,16]{1,0:T(8,128)} %wind_ref.1) | copy-start | bytes 3076
  0.0 13.8 %copy-start.3 = (f32[12,128]{1,0:T(8,128)S(1)}, f32[12,128]{1,0:T(8,128)}, u32[]{:S(2)}) copy-start(f32[12,128]{1,0:T(8,128)} %diff_ref.1) | copy-start | bytes 18436
  2.1 9.5 %collective-permute-start = (f32[12,16,128]{2,0,1:T(8,128)S(1)}, f32[12,16,128]{2,0,1:T(8,128)S(1)}, u32[]{:S(2)}, u32[]{:S(2)}) collective-permute-start(f32[12,16,128]{2,0,1:T(8,128)S(1)} %get-tuple-element.24), channel_id=1, source_target_pairs={{0,8},{8,16},{16,24},{24,0},{1,9},{9,17},{17,25},{25,1},{2,10},{10... | collective-permute-start | bytes 294920 | tf_op jit(solution)/shard_map/ppermute | solution.py:312
  5.2 7.8 %collective-permute-start.1 = (f32[12,16,128]{2,0,1:T(8,128)S(1)}, f32[12,16,128]{2,0,1:T(8,128)S(1)}, u32[]{:S(2)}, u32[]{:S(2)}) collective-permute-start(f32[12,16,128]{2,0,1:T(8,128)S(1)} %get-tuple-element.23), channel_id=1, source_target_pairs={{8,0},{16,8},{24,16},{0,24},{9,1},{17,9},{25,17},{1,25},{10,2},{18... | collective-permute-start | bytes 294920 | tf_op jit(solution)/shard_map/ppermute | solution.py:313
  7.3 5.7 %collective-permute-start.2 = (f32[16,12,128]{2,1,0:T(8,128)S(1)}, f32[16,12,128]{2,1,0:T(8,128)S(1)}, u32[]{:S(2)}, u32[]{:S(2)}) collective-permute-start(f32[16,12,128]{2,1,0:T(8,128)S(1)} %get-tuple-element.22), channel_id=1, source_target_pairs={{0,1},{1,2},{2,3},{3,4},{4,5},{5,6},{6,7},{8,9},{9,10},{10,11},{11... | collective-permute-start | bytes 294920 | tf_op jit(solution)/shard_map/ppermute | solution.py:315
  8.8 4.9 %collective-permute-start.3 = (f32[16,12,128]{2,1,0:T(8,128)S(1)}, f32[16,12,128]{2,1,0:T(8,128)S(1)}, u32[]{:S(2)}, u32[]{:S(2)}) collective-permute-start(f32[16,12,128]{2,1,0:T(8,128)S(1)} %get-tuple-element.21), channel_id=1, source_target_pairs={{1,0},{2,1},{3,2},{4,3},{5,4},{6,5},{7,6},{9,8},{10,9},{11,10},{12... | collective-permute-start | bytes 294920 | tf_op jit(solution)/shard_map/ppermute | solution.py:316
  13.8 33.9 %copy-start.1 = (bf16[1,1536,1024]{2,1,0:T(8,128)(2,1)S(1)}, bf16[1,1536,1024]{2,1,0:T(8,128)(2,1)}, u32[]{:S(2)}) copy-start(bf16[1,1536,1024]{2,1,0:T(8,128)(2,1)} %param.18) | copy-start | bytes 9437188
  13.8 33.9 %copy-start.2 = (bf16[1,1024,512]{2,1,0:T(8,128)(2,1)S(1)}, bf16[1,1024,512]{2,1,0:T(8,128)(2,1)}, u32[]{:S(2)}) copy-start(bf16[1,1024,512]{2,1,0:T(8,128)(2,1)} %param.23) | copy-start | bytes 3145732
  13.8 33.9 %copy-start.4 = (f32[1,2,1024]{2,1,0:T(2,128)S(1)}, f32[1,2,1024]{2,1,0:T(2,128)}, u32[]{:S(2)}) copy-start(f32[1,2,1024]{2,1,0:T(2,128)} %param.22) | copy-start | bytes 24580
  13.8 33.9 %copy-start.7 = (f32[1,1024]{1,0:T(1,128)S(1)}, f32[1,1024]{1,0:T(1,128)}, u32[]{:S(2)}) copy-start(f32[1,1024]{1,0:T(1,128)} %b_first.1) | copy-start | bytes 12292
  13.8 33.9 %copy-start.8 = (f32[1,1024]{1,0:T(1,128)S(1)}, f32[1,1024]{1,0:T(1,128)}, u32[]{:S(2)}) copy-start(f32[1,1024]{1,0:T(1,128)} %land_add.1) | copy-start | bytes 12292

commit v2 on v1

--- a/solution.py
+++ b/solution.py
@@ -10,8 +10,10 @@
 
 F32 = jnp.float32
 BF16 = jnp.bfloat16
+FIRST_PARTS = 3
 VM = pl.BlockSpec(memory_space=pltpu.VMEM)
 SM = pl.BlockSpec(memory_space=pltpu.SMEM)
+HB = pl.BlockSpec(memory_space=pltpu.HBM)
 
 
 class Plan:
@@ -105,10 +107,38 @@
     flags_ref[...] = jnp.dot(owner_hot, marked, preferred_element_type=F32)
 
 
+def band_place():
+    number = lax.axis_index("lat") * lax.axis_size("emu") + lax.axis_index("emu")
+    return lax.rem(number, 2) == 0
+
+
+def edge_kernel(*refs):
+    *refs, top_ref, bottom_ref, inner_ref, outer_ref, sems = refs
+    half = len(refs) // 2
+    copies = [
+        pltpu.make_async_copy(source, target, sems.at[k])
+        for k, (source, target) in enumerate(zip(refs[:half], refs[half:]))
+    ]
+    for copy in copies:
+        copy.start()
+    copies[0].wait()
+    state_ref = refs[half]
+    lats = state_ref.shape[2]
+    top_ref[...] = state_ref[state_ref.shape[0] - 1]
+    bottom_ref[...] = state_ref[0]
+    first, last = state_ref[:, :, 0, :], state_ref[:, :, lats - 1, :]
+    even = band_place()
+    inner_ref[...] = jnp.where(even, last, first)
+    outer_ref[...] = jnp.where(even, first, last)
+    for copy in copies[1:]:
+        copy.wait()
+
+
 def stencil_kernel(
-    plan, state_ref, west_ref, east_ref, south_ref, north_ref, diff_ref, wind_ref, flags_ref, *refs
+    plan, state_ref, west_ref, east_ref, inner_ref, outer_ref, diff_ref, wind_ref, flags_ref, *refs
 ):
     refs = list(refs)
+    even = band_place()
     pack_full = refs.pop(0) if plan.full else None
     pack_rest = refs.pop(0) if plan.rest else None
     out_ref, kept_ref, feature_ref = refs
@@ -123,13 +153,15 @@
             center = state_ref[lon, number]
             east = state_ref[lon + 1, number] if lon + 1 < lons else east_ref[number]
             west = state_ref[lon - 1, number] if lon else west_ref[number]
+            inner = inner_ref[lon, number : number + 1, :]
+            outer = outer_ref[lon, number : number + 1, :]
             north = jnp.where(
                 row == lats - 1,
-                north_ref[lon, number : number + 1, :],
+                jnp.where(even, inner, outer),
                 pltpu.roll(center, lats - 1, 0),
             )
             south = jnp.where(
-                row == 0, south_ref[lon, number : number + 1, :], pltpu.roll(center, 1, 0)
+                row == 0, jnp.where(even, outer, inner), pltpu.roll(center, 1, 0)
             )
             total = east + west + north + south - 4.0 * center
             half = wind_ref[lon * lats : (lon + 1) * lats, :]
@@ -170,9 +202,34 @@
 
 
 def network_kernel(
-    plan, rows_ref, w_first, b_first, land_add, w_inner, b_inner, w_last, out_ref, x_ref
+    plan,
+    rows_ref,
+    b_first,
+    land_add,
+    b_inner,
+    first_hbm,
+    inner_hbm,
+    last_hbm,
+    out_ref,
+    x_ref,
+    w_first,
+    w_inner,
+    w_last,
+    sems,
 ):
     sources, _, levels = rows_ref.shape
+    step = w_first.shape[0] // FIRST_PARTS
+    parts = [slice(k * step, (k + 1) * step) for k in range(FIRST_PARTS)]
+    pairs = [(first_hbm.at[part], w_first.at[part]) for part in parts]
+    pairs += [(inner_hbm.at[k], w_inner.at[k]) for k in range(w_inner.shape[0])]
+    pairs += [(last_hbm, w_last)]
+    copies = [
+        pltpu.make_async_copy(source, target, sems.at[k])
+        for k, (source, target) in enumerate(pairs)
+    ]
+    for copy in copies:
+        copy.start()
+    copies.reverse()
     variables = w_first.shape[0] // levels
     lead = sources * plan.full
     small = sources * plan.rest
@@ -210,11 +267,16 @@
         target, column = spread(plan, 0)
         flags.append(jnp.dot(hot(target == column), tall, preferred_element_type=F32)[:, :1])
     flag = jnp.concatenate(flags, axis=0)
-    pre = jnp.dot(x_ref[...], w_first[...], preferred_element_type=F32) + b_first[...]
+    pre = jnp.broadcast_to(b_first[...], (x_ref.shape[0], b_first.shape[1]))
+    for part in parts:
+        copies.pop().wait()
+        pre += jnp.dot(x_ref[:, part], w_first[part, :], preferred_element_type=F32)
     hidden = jax.nn.silu(pre + flag * land_add[...]).astype(BF16)
     for number in range(w_inner.shape[0]):
+        copies.pop().wait()
         pre = jnp.dot(hidden, w_inner[number], preferred_element_type=F32)
         hidden = jax.nn.silu(pre + b_inner[number : number + 1, :]).astype(BF16)
+    copies.pop().wait()
     made = jnp.dot(hidden, w_last[...], preferred_element_type=F32).astype(BF16)
     outs = made.shape[1] // levels
     if plan.full:
@@ -290,14 +352,14 @@
         out_ref[pl.ds(number, columns, stride=outs), :] = base + found[number]
 
 
-def call(kernel, specs, shapes, scratch=()):
+def call(kernel, specs, shapes, scratch=(), room=12):
     return pl.pallas_call(
         kernel,
         in_specs=specs,
         out_specs=jax.tree.map(lambda _: VM, shapes),
         out_shape=shapes,
         scratch_shapes=list(scratch),
-        compiler_params=pltpu.CompilerParams(vmem_limit_bytes=48 * 1024 * 1024),
+        compiler_params=pltpu.CompilerParams(vmem_limit_bytes=room * 1024 * 1024),
     )
 
 
@@ -305,16 +367,32 @@
     return jax.ShapeDtypeStruct(tuple(dims), dtype)
 
 
-def exchanged(state):
+def far(values):
+    return pltpu.with_memory_space_constraint(values, pltpu.HBM)
+
+
+def exchanged(state, *others):
+    lons, variables, lats, levels = state.shape
+    lon_edge = shape((variables, lats, levels), F32)
+    lat_edge = shape((lons, variables, levels), F32)
+    values = (state,) + others
+    *values, top, bottom, inner, outer = call(
+        edge_kernel,
+        [HB] * len(values),
+        [shape(v.shape, v.dtype) for v in values] + [lon_edge, lon_edge, lat_edge, lat_edge],
+        [pltpu.SemaphoreType.DMA((len(values),))],
+    )(*[far(v) for v in values])
     tiles = lax.axis_size("tile")
     bands = lax.axis_size("lat") * lax.axis_size("emu")
     up = [(i, (i + 1) % tiles) for i in range(tiles)]
-    west = lax.ppermute(state[-1], "tile", up)
-    east = lax.ppermute(state[0], "tile", [(b, a) for a, b in up])
-    along = [(i, i + 1) for i in range(bands - 1)]
-    south = lax.ppermute(state[:, :, -1, :], ("lat", "emu"), along)
-    north = lax.ppermute(state[:, :, 0, :], ("lat", "emu"), [(b, a) for a, b in along])
-    return west, east, south, north
+
+    def swap(values, start):
+        pairs = [(i, i + 1) for i in range(start, bands - 1, 2)]
+        return lax.ppermute(values, ("lat", "emu"), pairs + [(b, a) for a, b in pairs])
+
+    west = lax.ppermute(top, "tile", up)
+    east = lax.ppermute(bottom, "tile", [(b, a) for a, b in up])
+    return values, (west, east, swap(inner, 0), swap(outer, 1))
 
 
 def body(
@@ -327,7 +405,9 @@
     capacity = max(2, columns * 5 // (4 * experts))
     plan = Plan(experts, capacity)
     state = jnp.transpose(state, (0, 2, 1, 3))
-    halos = exchanged(state)
+    (state, diffusivity, wind, land_mask, routes), halos = exchanged(
+        state, diffusivity, wind, land_mask, routes.reshape(1, columns)
+    )
 
     shapes = [shape((experts, levels), F32), shape((columns, levels), F32)]
     if plan.full:
@@ -344,7 +424,7 @@
         [SM, VM, VM, VM],
         shapes,
         [pltpu.VMEM((columns, levels), F32)],
-    )(counts.reshape(1, 1), routes.reshape(1, columns), land_mask, wind)
+    )(counts.reshape(1, 1), routes, land_mask, wind)
     flags, half_wind = made[:2]
     packs, picks = made[2::2], made[3::2]
 
@@ -362,10 +442,17 @@
     rows = lax.all_to_all(rows, axes, split_axis=0, concat_axis=0, tiled=True)
     made = call(
         functools.partial(network_kernel, plan),
-        [VM] * 7,
+        [VM] * 4 + [HB] * 3,
         shape((experts, plan.rows(outs), levels), BF16),
-        [pltpu.VMEM((experts * capacity, variables * levels), BF16)],
-    )(rows, w_in[0], b_in, land_vec, w_hid[0], b_hid[0], w_out[0])
+        [
+            pltpu.VMEM((experts * capacity, variables * levels), BF16),
+            pltpu.VMEM(w_in.shape[1:], BF16),
+            pltpu.VMEM(w_hid.shape[1:], BF16),
+            pltpu.VMEM(w_out.shape[1:], BF16),
+            pltpu.SemaphoreType.DMA((FIRST_PARTS + w_hid.shape[1] + 1,)),
+        ],
+        32,
+    )(rows, b_in, land_vec, b_hid[0], far(w_in[0]), far(w_hid[0]), far(w_out[0]))
     made = lax.all_to_all(made, axes, split_axis=0, concat_axis=0, tiled=True)
     out = call(
         functools.partial(finish_kernel, plan),

time: 70.7 us -> 67.6 us (0.956)
  local copies, waits for them, and re-layouts: 2.22 us -> 0.01 us
  starting transfers between devices: 7.97 us -> 5.86 us
  Pallas kernels: 8.28 us -> 9.91 us
    ppermute x4, starting transfers between devices: 7.97 us -> 5.86 us  [the longest x1 3.1 us: exchanged(): west = lax.ppermute(top, 'tile', up)]
    unnamed x21 -> x6, local copies, waits for them, and re-layouts: 2.11 us -> 0.01 us
    all_to_all x1, blocking collectives: 16.3 us -> 14.2 us  [body(): made = lax.all_to_all(made, axes, split_axis=0, concat_axis=0, tiled=True)]
    all_to_all x1, blocking collectives: 32.5 us -> 34.1 us  [body(): rows = lax.all_to_all(rows, axes, split_axis=0, concat_axis=0, tiled=True)]
    pallas_call x1 -> x2, Pallas kernels: 5.38 us -> 6.93 us  [the longest x1 5.22 us: body(): call(functools.partial(network_kernel, plan), [VM] * 4 + [HB] * 3, shape(...]
  transfers between devices with their start and end apart: 4 -> 4, of which waited for: 3 -> 2; matrix products, arithmetic and copies ran while one was open for 0% -> 0% of each run, Pallas kernels for 1% -> 1%
where the time goes in v2:
time: 67.6 us; the launch traced here: 67.3 us
  blocking collectives  48.4 us (72%)
  Pallas kernels  9.91 us (15%)
  starting transfers between devices  5.86 us (9%)
  waiting for transfers between devices  2.51 us (4%)
  between operations  0.7 us (1%)
    all_to_all x1, blocking collectives, body(): rows = lax.all_to_all(rows, axes, split_axis=0, concat_axis=0, tiled=True)  34.1 us
    all_to_all x1, blocking collectives, body(): made = lax.all_to_all(made, axes, split_axis=0, concat_axis=0, tiled=True)  14.2 us
    pallas_call x1, Pallas kernels, body(): call(functools.partial(network_kernel, plan), [VM] * 4 + [HB] * 3, shape(...  5.22 us
    ppermute x1, starting transfers between devices, exchanged(): west = lax.ppermute(top, 'tile', up)  3.1 us
    ppermute x1, starting transfers between devices, exchanged(): east = lax.ppermute(bottom, 'tile', [(b, a) for a, b in up])  2.09 us
    pallas_call x1, Pallas kernels, exchanged(): call(edge_kernel, [HB] * len(values), [shape(v.shape, v.dtype) for v in v...  1.7 us
    ppermute x1, waiting for transfers between devices, exchanged(): west = lax.ppermute(top, 'tile', up)  1.61 us
    pallas_call x1, Pallas kernels, body(): call(functools.partial(stencil_kernel, plan), [VM] * (8 + len(packs)), [s...  1.44 us
  transfers between devices with their start and end apart: 4, of which 2 were waited for; matrix products, arithmetic and copies ran while one was open for 0% of the time, Pallas kernels for 1%

profile of v2, /device:TPU:0, one launch (start us, length us, event | category | flops | bytes accessed | tf_op | source)
XLA Modules:
  0.0 67.3 jit_solution(16056376445575132047)
XLA Ops:
  0.0 0.0 copy-start
  0.0 0.0 copy-start.2
  0.0 0.0 copy-start.1
  0.0 1.7 %shard_map.118 = (f32[16,12,16,128]{3,2,1,0:T(8,128)S(1)}, f32[12,128]{1,0:T(8,128)S(1)}, f32[16,16]{1,0:T(8,128)S(1)}, s32[16,16]{1,0:T(8,128)S(1)}, s32[1,256]...) custom-call(f32[16,12,16,128]{3,2,1,0:T(8,128)} %bitcast.12, ...), custom_call_target="tpu_custom_call" | custom-call | tf_op jit(solution)/shard_map/pallas_call | solution.py:379
  1.7 3.1 %collective-permute-start = (f32[12,16,128]{2,1,0:T(8,128)S(1)}, f32[12,16,128]{2,1,0:T(8,128)S(1)}, u32[]{:S(2)}, u32[]{:S(2)}) collective-permute-start(f32[12,16,128]{2,1,0:T(8,128)S(1)} %get-tuple-element.23), channel_id=1, source_target_pairs={{0,8},{8,16},{16,24},{24,0},{1,9},{9,17},{17,25},{25,1},{2,10},{10... | collective-permute-start | bytes 294920 | tf_op jit(solution)/shard_map/ppermute | solution.py:393
  4.8 2.1 %collective-permute-start.1 = (f32[12,16,128]{2,1,0:T(8,128)S(1)}, f32[12,16,128]{2,1,0:T(8,128)S(1)}, u32[]{:S(2)}, u32[]{:S(2)}) collective-permute-start(f32[12,16,128]{2,1,0:T(8,128)S(1)} %get-tuple-element.24), channel_id=1, source_target_pairs={{8,0},{16,8},{24,16},{0,24},{9,1},{17,9},{25,17},{1,25},{10,2},{18... | collective-permute-start | bytes 294920 | tf_op jit(solution)/shard_map/ppermute | solution.py:394
  6.9 0.0 collective-permute-start.2
  6.9 0.7 collective-permute-start.3
  8.2 0.4 shard_map.119
  8.7 1.6 %collective-permute-done.west_ref = f32[12,16,128]{2,1,0:T(8,128)S(1)} collective-permute-done((f32[12,16,128]{2,1,0:T(8,128)S(1)}, f32[12,16,128]{2,1,0:T(8,128)S(1)}, u32[]{:S(2)}, u32[]{:S(2)}) %collective-permute-start) | collective-permute-done | bytes 98336 | tf_op jit(solution)/shard_map/ppermute | solution.py:393
  10.3 0.9 %collective-permute-done.1.east_ref = f32[12,16,128]{2,1,0:T(8,128)S(1)} collective-permute-done((f32[12,16,128]{2,1,0:T(8,128)S(1)}, f32[12,16,128]{2,1,0:T(8,128)S(1)}, u32[]{:S(2)}, u32[]{:S(2)}) %collective-permute-start.1) | collective-permute-done | bytes 98336 | tf_op jit(solution)/shard_map/ppermute | solution.py:394
  11.2 0.0 collective-permute-done.2.inner_ref
  11.2 0.0 collective-permute-done.3.outer_ref
  11.2 1.4 %shard_map.120 = (bf16[16,248,128]{2,1,0:T(8,128)(2,1)S(1)}, f32[16,4,16,128]{3,2,1,0:T(8,128)S(1)}) custom-call(f32[16,12,16,128]{3,2,1,0:T(8,128)S(1)} %get-tuple-element.22.state_ref, f32[12,16,128]{2,1,0:T(8,128)S(1)} %collective-permute-done.west_ref, f32[12,16,128]{2,1,0:T(8,128)S(1)} %collective-permute-done.1.east_ref, ...), custom_call_target="tpu_custom_call" | custom-call | tf_op jit(solution)/shard_map/pallas_call | solution.py:431
  12.6 34.1 %all_to_all.10.rows_ref = bf16[16,248,128]{2,1,0:T(8,128)(2,1)S(1)} all-to-all(bf16[16,248,128]{2,1,0:T(8,128)(2,1)S(1)} %get-tuple-element.35), channel_id=1, replica_groups=mesh['tile'=4,'lat'=4,'emu'=2] {'tile','lat'}, dimensions={0} | all-to-all | bytes 2031616 | tf_op jit(solution)/shard_map/all_to_all | solution.py:442
  46.8 0.0 copy-done
  46.8 0.0 copy-done.2
  46.8 0.0 copy-done.1
  46.8 5.2 %shard_map.121 = bf16[16,80,128]{2,1,0:T(8,128)(2,1)S(1)} custom-call(bf16[16,248,128]{2,1,0:T(8,128)(2,1)S(1)} %all_to_all.10.rows_ref, f32[1,1024]{1,0:T(1,128)S(1)} %copy-done.1, f32[1,1024]{1,0:T(1,128)S(1)} %copy-done.2, f32[2,1024]{1,0:T(2,128)S(1)} %bitcast.9, bf16[1536,1024]{1,0:T(8,128)(2,1)} %bitcast.11, bf16[2,1024,1024]{2,1,0:T(8,128)(2,1)} %bitcast.10, ...), custom_call_target="tpu_custom_call" | custom-call | tf_op jit(solution)/shard_map/pallas_call | solution.py:443
  52.0 14.2 %all_to_all.11.rows_ref = bf16[16,80,128]{2,1,0:T(8,128)(2,1)S(1)} all-to-all(bf16[16,80,128]{2,1,0:T(8,128)(2,1)S(1)} %shard_map.121), channel_id=1, replica_groups=mesh['tile'=4,'lat'=4,'emu'=2] {'tile','lat'}, dimensions={0} | all-to-all | bytes 655360 | tf_op jit(solution)/shard_map/all_to_all | solution.py:456
  66.3 1.1 %shard_map.122 = f32[1024,128]{1,0:T(8,128)} custom-call(bf16[16,80,128]{2,1,0:T(8,128)(2,1)S(1)} %all_to_all.11.rows_ref, f32[16,4,16,128]{3,2,1,0:T(8,128)S(1)} %get-tuple-element.36.kept_ref, bf16[256,256]{1,0:T(8,128)(2,1)S(1)} %get-tuple-element.37.refs_0_, bf16[256,256]{1,0:T(8,128)(2,1)S(1)} %get-tuple-element.38.refs_1_), custom_call_target="tpu_custom_call" | custom-call | tf_op jit(solution)/shard_map/pallas_call | solution.py:457
Async XLA Ops:
  0.0 46.8 %copy-start = (f32[1,2,1024]{2,1,0:T(2,128)S(1)}, f32[1,2,1024]{2,1,0:T(2,128)}, u32[]{:S(2)}) copy-start(f32[1,2,1024]{2,1,0:T(2,128)} %param.22) | copy-start | bytes 24580
  0.0 46.8 %copy-start.2 = (f32[1,1024]{1,0:T(1,128)S(1)}, f32[1,1024]{1,0:T(1,128)}, u32[]{:S(2)}) copy-start(f32[1,1024]{1,0:T(1,128)} %land_add.1) | copy-start | bytes 12292
  0.0 46.8 %copy-start.1 = (f32[1,1024]{1,0:T(1,128)S(1)}, f32[1,1024]{1,0:T(1,128)}, u32[]{:S(2)}) copy-start(f32[1,1024]{1,0:T(1,128)} %b_first.1) | copy-start | bytes 12292
  1.7 8.6 %collective-permute-start = (f32[12,16,128]{2,1,0:T(8,128)S(1)}, f32[12,16,128]{2,1,0:T(8,128)S(1)}, u32[]{:S(2)}, u32[]{:S(2)}) collective-permute-start(f32[12,16,128]{2,1,0:T(8,128)S(1)} %get-tuple-element.23), channel_id=1, source_target_pairs={{0,8},{8,16},{16,24},{24,0},{1,9},{9,17},{17,25},{25,1},{2,10},{10... | collective-permute-start | bytes 294920 | tf_op jit(solution)/shard_map/ppermute | solution.py:393
  4.8 6.4 %collective-permute-start.1 = (f32[12,16,128]{2,1,0:T(8,128)S(1)}, f32[12,16,128]{2,1,0:T(8,128)S(1)}, u32[]{:S(2)}, u32[]{:S(2)}) collective-permute-start(f32[12,16,128]{2,1,0:T(8,128)S(1)} %get-tuple-element.24), channel_id=1, source_target_pairs={{8,0},{16,8},{24,16},{0,24},{9,1},{17,9},{25,17},{1,25},{10,2},{18... | collective-permute-start | bytes 294920 | tf_op jit(solution)/shard_map/ppermute | solution.py:394
  6.9 4.3 %collective-permute-start.2 = (f32[16,12,128]{2,1,0:T(8,128)S(1)}, f32[16,12,128]{2,1,0:T(8,128)S(1)}, u32[]{:S(2)}, u32[]{:S(2)}) collective-permute-start(f32[16,12,128]{2,1,0:T(8,128)S(1)} %get-tuple-element.25), channel_id=1, source_target_pairs={{0,1},{2,3},{4,5},{6,7},{1,0},{3,2},{5,4},{7,6},{8,9},{10,11},{12,... | collective-permute-start | bytes 294920 | tf_op jit(solution)/shard_map/ppermute | solution.py:391
  6.9 4.3 %collective-permute-start.3 = (f32[16,12,128]{2,1,0:T(8,128)S(1)}, f32[16,12,128]{2,1,0:T(8,128)S(1)}, u32[]{:S(2)}, u32[]{:S(2)}) collective-permute-start(f32[16,12,128]{2,1,0:T(8,128)S(1)} %get-tuple-element.26), channel_id=1, source_target_pairs={{1,2},{3,4},{5,6},{2,1},{4,3},{6,5},{9,10},{11,12},{13,14},{10,9},... | collective-permute-start | bytes 294920 | tf_op jit(solution)/shard_map/ppermute | solution.py:391

commit v3 on v2

--- a/solution.py
+++ b/solution.py
@@ -10,7 +10,6 @@
 
 F32 = jnp.float32
 BF16 = jnp.bfloat16
-FIRST_PARTS = 3
 VM = pl.BlockSpec(memory_space=pltpu.VMEM)
 SM = pl.BlockSpec(memory_space=pltpu.SMEM)
 HB = pl.BlockSpec(memory_space=pltpu.HBM)
@@ -207,21 +206,17 @@
     b_first,
     land_add,
     b_inner,
-    first_hbm,
+    w_first,
     inner_hbm,
     last_hbm,
     out_ref,
     x_ref,
-    w_first,
     w_inner,
     w_last,
     sems,
 ):
     sources, _, levels = rows_ref.shape
-    step = w_first.shape[0] // FIRST_PARTS
-    parts = [slice(k * step, (k + 1) * step) for k in range(FIRST_PARTS)]
-    pairs = [(first_hbm.at[part], w_first.at[part]) for part in parts]
-    pairs += [(inner_hbm.at[k], w_inner.at[k]) for k in range(w_inner.shape[0])]
+    pairs = [(inner_hbm.at[k], w_inner.at[k]) for k in range(w_inner.shape[0])]
     pairs += [(last_hbm, w_last)]
     copies = [
         pltpu.make_async_copy(source, target, sems.at[k])
@@ -267,10 +262,7 @@
         target, column = spread(plan, 0)
         flags.append(jnp.dot(hot(target == column), tall, preferred_element_type=F32)[:, :1])
     flag = jnp.concatenate(flags, axis=0)
-    pre = jnp.broadcast_to(b_first[...], (x_ref.shape[0], b_first.shape[1]))
-    for part in parts:
-        copies.pop().wait()
-        pre += jnp.dot(x_ref[:, part], w_first[part, :], preferred_element_type=F32)
+    pre = jnp.dot(x_ref[...], w_first[...], preferred_element_type=F32) + b_first[...]
     hidden = jax.nn.silu(pre + flag * land_add[...]).astype(BF16)
     for number in range(w_inner.shape[0]):
         copies.pop().wait()
@@ -390,9 +382,11 @@
         pairs = [(i, i + 1) for i in range(start, bands - 1, 2)]
         return lax.ppermute(values, ("lat", "emu"), pairs + [(b, a) for a, b in pairs])
 
+    outer = swap(outer, 1)
     west = lax.ppermute(top, "tile", up)
     east = lax.ppermute(bottom, "tile", [(b, a) for a, b in up])
-    return values, (west, east, swap(inner, 0), swap(outer, 1))
+    inner = swap(inner, 0)
+    return values, (west, east, inner, outer)
 
 
 def body(
@@ -442,17 +436,16 @@
     rows = lax.all_to_all(rows, axes, split_axis=0, concat_axis=0, tiled=True)
     made = call(
         functools.partial(network_kernel, plan),
-        [VM] * 4 + [HB] * 3,
+        [VM] * 5 + [HB] * 2,
         shape((experts, plan.rows(outs), levels), BF16),
         [
             pltpu.VMEM((experts * capacity, variables * levels), BF16),
-            pltpu.VMEM(w_in.shape[1:], BF16),
             pltpu.VMEM(w_hid.shape[1:], BF16),
             pltpu.VMEM(w_out.shape[1:], BF16),
-            pltpu.SemaphoreType.DMA((FIRST_PARTS + w_hid.shape[1] + 1,)),
+            pltpu.SemaphoreType.DMA((w_hid.shape[1] + 1,)),
         ],
         32,
-    )(rows, b_in, land_vec, b_hid[0], far(w_in[0]), far(w_hid[0]), far(w_out[0]))
+    )(rows, b_in, land_vec, b_hid[0], w_in[0], far(w_hid[0]), far(w_out[0]))
     made = lax.all_to_all(made, axes, split_axis=0, concat_axis=0, tiled=True)
     out = call(
         functools.partial(finish_kernel, plan),

time: 67.6 us -> 66.9 us (0.990)
  Pallas kernels: 9.91 us -> 9.16 us
    pallas_call x1, Pallas kernels: 5.22 us -> 4.37 us  [body(): call(functools.partial(network_kernel, plan), [VM] * 5 + [HB] * 2, shape(...]
where the time goes in v3:
time: 66.9 us; the launch traced here: 66.6 us
  blocking collectives  48.4 us (72%)
  Pallas kernels  9.16 us (14%)
  starting transfers between devices  5.87 us (9%)
  waiting for transfers between devices  2.51 us (4%)
  between operations  0.7 us (1%)
    all_to_all x1, blocking collectives, body(): rows = lax.all_to_all(rows, axes, split_axis=0, concat_axis=0, tiled=True)  34.2 us
    all_to_all x1, blocking collectives, body(): made = lax.all_to_all(made, axes, split_axis=0, concat_axis=0, tiled=True)  14.2 us
    pallas_call x1, Pallas kernels, body(): call(functools.partial(network_kernel, plan), [VM] * 5 + [HB] * 2, shape(...  4.37 us
    ppermute x1, starting transfers between devices, exchanged(): west = lax.ppermute(top, 'tile', up)  3.12 us
    ppermute x1, starting transfers between devices, exchanged(): east = lax.ppermute(bottom, 'tile', [(b, a) for a, b in up])  2.09 us
    pallas_call x1, Pallas kernels, exchanged(): call(edge_kernel, [HB] * len(values), [shape(v.shape, v.dtype) for v in v...  1.81 us
    ppermute x1, waiting for transfers between devices, exchanged(): west = lax.ppermute(top, 'tile', up)  1.61 us
    pallas_call x1, Pallas kernels, body(): call(functools.partial(stencil_kernel, plan), [VM] * (8 + len(packs)), [s...  1.44 us
  transfers between devices with their start and end apart: 4, of which 2 were waited for; matrix products, arithmetic and copies ran while one was open for 0% of the time, Pallas kernels for 1%

profile of v3, /device:TPU:0, one launch (start us, length us, event | category | flops | bytes accessed | tf_op | source)
XLA Modules:
  0.0 66.6 jit_solution(16437010961520645271)
XLA Ops:
  0.0 0.0 copy-start.1
  0.0 0.0 copy-start.3
  0.0 0.0 copy-start.2
  0.0 0.0 copy-start
  0.0 1.8 %shard_map.118 = (f32[16,12,16,128]{3,2,1,0:T(8,128)S(1)}, f32[12,128]{1,0:T(8,128)S(1)}, f32[16,16]{1,0:T(8,128)S(1)}, s32[16,16]{1,0:T(8,128)S(1)}, s32[1,256]...) custom-call(f32[16,12,16,128]{3,2,1,0:T(8,128)} %bitcast.12, ...), custom_call_target="tpu_custom_call" | custom-call | tf_op jit(solution)/shard_map/pallas_call | solution.py:371
  1.8 3.1 %collective-permute-start = (f32[12,16,128]{2,1,0:T(8,128)S(1)}, f32[12,16,128]{2,1,0:T(8,128)S(1)}, u32[]{:S(2)}, u32[]{:S(2)}) collective-permute-start(f32[12,16,128]{2,1,0:T(8,128)S(1)} %get-tuple-element.23), channel_id=1, source_target_pairs={{0,8},{8,16},{16,24},{24,0},{1,9},{9,17},{17,25},{25,1},{2,10},{10... | collective-permute-start | bytes 294920 | tf_op jit(solution)/shard_map/ppermute | solution.py:386
  4.9 2.1 %collective-permute-start.1 = (f32[12,16,128]{2,1,0:T(8,128)S(1)}, f32[12,16,128]{2,1,0:T(8,128)S(1)}, u32[]{:S(2)}, u32[]{:S(2)}) collective-permute-start(f32[12,16,128]{2,1,0:T(8,128)S(1)} %get-tuple-element.24), channel_id=1, source_target_pairs={{8,0},{16,8},{24,16},{0,24},{9,1},{17,9},{25,17},{1,25},{10,2},{18... | collective-permute-start | bytes 294920 | tf_op jit(solution)/shard_map/ppermute | solution.py:387
  7.0 0.0 collective-permute-start.2
  7.0 0.7 collective-permute-start.3
  8.4 0.4 shard_map.119
  8.8 1.6 %collective-permute-done.west_ref = f32[12,16,128]{2,1,0:T(8,128)S(1)} collective-permute-done((f32[12,16,128]{2,1,0:T(8,128)S(1)}, f32[12,16,128]{2,1,0:T(8,128)S(1)}, u32[]{:S(2)}, u32[]{:S(2)}) %collective-permute-start) | collective-permute-done | bytes 98336 | tf_op jit(solution)/shard_map/ppermute | solution.py:386
  10.4 0.9 %collective-permute-done.1.east_ref = f32[12,16,128]{2,1,0:T(8,128)S(1)} collective-permute-done((f32[12,16,128]{2,1,0:T(8,128)S(1)}, f32[12,16,128]{2,1,0:T(8,128)S(1)}, u32[]{:S(2)}, u32[]{:S(2)}) %collective-permute-start.1) | collective-permute-done | bytes 98336 | tf_op jit(solution)/shard_map/ppermute | solution.py:387
  11.3 0.0 collective-permute-done.2.inner_ref
  11.3 0.0 collective-permute-done.3.outer_ref
  11.3 1.4 %shard_map.120 = (bf16[16,248,128]{2,1,0:T(8,128)(2,1)S(1)}, f32[16,4,16,128]{3,2,1,0:T(8,128)S(1)}) custom-call(f32[16,12,16,128]{3,2,1,0:T(8,128)S(1)} %get-tuple-element.22.state_ref, f32[12,16,128]{2,1,0:T(8,128)S(1)} %collective-permute-done.west_ref, f32[12,16,128]{2,1,0:T(8,128)S(1)} %collective-permute-done.1.east_ref, ...), custom_call_target="tpu_custom_call" | custom-call | tf_op jit(solution)/shard_map/pallas_call | solution.py:425
  12.8 34.2 %all_to_all.10.rows_ref = bf16[16,248,128]{2,1,0:T(8,128)(2,1)S(1)} all-to-all(bf16[16,248,128]{2,1,0:T(8,128)(2,1)S(1)} %get-tuple-element.35), channel_id=1, replica_groups=mesh['tile'=4,'lat'=4,'emu'=2] {'tile','lat'}, dimensions={0} | all-to-all | bytes 2031616 | tf_op jit(solution)/shard_map/all_to_all | solution.py:436
  46.9 0.0 copy-done.1
  46.9 0.0 copy-done.3
  46.9 0.0 copy-done.2
  46.9 0.0 copy-done
  46.9 4.4 %shard_map.121 = bf16[16,80,128]{2,1,0:T(8,128)(2,1)S(1)} custom-call(bf16[16,248,128]{2,1,0:T(8,128)(2,1)S(1)} %all_to_all.10.rows_ref, f32[1,1024]{1,0:T(1,128)S(1)} %copy-done.2, f32[1,1024]{1,0:T(1,128)S(1)} %copy-done.3, f32[2,1024]{1,0:T(2,128)S(1)} %bitcast.10, bf16[1536,1024]{1,0:T(8,128)(2,1)S(1)} %bitcast.9, bf16[2,1024,1024]{2,1,0:T(8,128)(2,1)} %bitcast.11, ...), custom_call_target="tpu_custom_call" | custom-call | tf_op jit(solution)/shard_map/pallas_call | solution.py:437
  51.3 14.2 %all_to_all.11.rows_ref = bf16[16,80,128]{2,1,0:T(8,128)(2,1)S(1)} all-to-all(bf16[16,80,128]{2,1,0:T(8,128)(2,1)S(1)} %shard_map.121), channel_id=1, replica_groups=mesh['tile'=4,'lat'=4,'emu'=2] {'tile','lat'}, dimensions={0} | all-to-all | bytes 655360 | tf_op jit(solution)/shard_map/all_to_all | solution.py:449
  65.5 1.1 %shard_map.122 = f32[1024,128]{1,0:T(8,128)} custom-call(bf16[16,80,128]{2,1,0:T(8,128)(2,1)S(1)} %all_to_all.11.rows_ref, f32[16,4,16,128]{3,2,1,0:T(8,128)S(1)} %get-tuple-element.36.kept_ref, bf16[256,256]{1,0:T(8,128)(2,1)S(1)} %get-tuple-element.37.refs_0_, bf16[256,256]{1,0:T(8,128)(2,1)S(1)} %get-tuple-element.38.refs_1_), custom_call_target="tpu_custom_call" | custom-call | tf_op jit(solution)/shard_map/pallas_call | solution.py:450
Async XLA Ops:
  0.0 46.9 %copy-start.1 = (f32[1,2,1024]{2,1,0:T(2,128)S(1)}, f32[1,2,1024]{2,1,0:T(2,128)}, u32[]{:S(2)}) copy-start(f32[1,2,1024]{2,1,0:T(2,128)} %param.22) | copy-start | bytes 24580
  0.0 46.9 %copy-start.3 = (f32[1,1024]{1,0:T(1,128)S(1)}, f32[1,1024]{1,0:T(1,128)}, u32[]{:S(2)}) copy-start(f32[1,1024]{1,0:T(1,128)} %land_add.1) | copy-start | bytes 12292
  0.0 46.9 %copy-start.2 = (f32[1,1024]{1,0:T(1,128)S(1)}, f32[1,1024]{1,0:T(1,128)}, u32[]{:S(2)}) copy-start(f32[1,1024]{1,0:T(1,128)} %b_first.1) | copy-start | bytes 12292
  0.0 46.9 %copy-start = (bf16[1,1536,1024]{2,1,0:T(8,128)(2,1)S(1)}, bf16[1,1536,1024]{2,1,0:T(8,128)(2,1)}, u32[]{:S(2)}) copy-start(bf16[1,1536,1024]{2,1,0:T(8,128)(2,1)} %param.18) | copy-start | bytes 9437188
  1.8 8.6 %collective-permute-start = (f32[12,16,128]{2,1,0:T(8,128)S(1)}, f32[12,16,128]{2,1,0:T(8,128)S(1)}, u32[]{:S(2)}, u32[]{:S(2)}) collective-permute-start(f32[12,16,128]{2,1,0:T(8,128)S(1)} %get-tuple-element.23), channel_id=1, source_target_pairs={{0,8},{8,16},{16,24},{24,0},{1,9},{9,17},{17,25},{25,1},{2,10},{10... | collective-permute-start | bytes 294920 | tf_op jit(solution)/shard_map/ppermute | solution.py:386
  4.9 6.4 %collective-permute-start.1 = (f32[12,16,128]{2,1,0:T(8,128)S(1)}, f32[12,16,128]{2,1,0:T(8,128)S(1)}, u32[]{:S(2)}, u32[]{:S(2)}) collective-permute-start(f32[12,16,128]{2,1,0:T(8,128)S(1)} %get-tuple-element.24), channel_id=1, source_target_pairs={{8,0},{16,8},{24,16},{0,24},{9,1},{17,9},{25,17},{1,25},{10,2},{18... | collective-permute-start | bytes 294920 | tf_op jit(solution)/shard_map/ppermute | solution.py:387
  7.0 4.3 %collective-permute-start.2 = (f32[16,12,128]{2,1,0:T(8,128)S(1)}, f32[16,12,128]{2,1,0:T(8,128)S(1)}, u32[]{:S(2)}, u32[]{:S(2)}) collective-permute-start(f32[16,12,128]{2,1,0:T(8,128)S(1)} %get-tuple-element.25), channel_id=1, source_target_pairs={{0,1},{2,3},{4,5},{6,7},{1,0},{3,2},{5,4},{7,6},{8,9},{10,11},{12,... | collective-permute-start | bytes 294920 | tf_op jit(solution)/shard_map/ppermute | solution.py:383
  7.0 4.3 %collective-permute-start.3 = (f32[16,12,128]{2,1,0:T(8,128)S(1)}, f32[16,12,128]{2,1,0:T(8,128)S(1)}, u32[]{:S(2)}, u32[]{:S(2)}) collective-permute-start(f32[16,12,128]{2,1,0:T(8,128)S(1)} %get-tuple-element.26), channel_id=1, source_target_pairs={{1,2},{3,4},{5,6},{2,1},{4,3},{6,5},{9,10},{11,12},{13,14},{10,9},... | collective-permute-start | bytes 294920 | tf_op jit(solution)/shard_map/ppermute | solution.py:383

commit v4 on v3

--- a/solution.py
+++ b/solution.py
@@ -112,7 +112,7 @@
 
 
 def edge_kernel(*refs):
-    *refs, top_ref, bottom_ref, inner_ref, outer_ref, sems = refs
+    *refs, outer_ref, top_ref, bottom_ref, inner_ref, sems = refs
     half = len(refs) // 2
     copies = [
         pltpu.make_async_copy(source, target, sems.at[k])
@@ -123,18 +123,18 @@
     copies[0].wait()
     state_ref = refs[half]
     lats = state_ref.shape[2]
-    top_ref[...] = state_ref[state_ref.shape[0] - 1]
-    bottom_ref[...] = state_ref[0]
+    top_ref[...] = state_ref[state_ref.shape[0] - 1].astype(BF16)
+    bottom_ref[...] = state_ref[0].astype(BF16)
     first, last = state_ref[:, :, 0, :], state_ref[:, :, lats - 1, :]
     even = band_place()
-    inner_ref[...] = jnp.where(even, last, first)
-    outer_ref[...] = jnp.where(even, first, last)
+    inner_ref[...] = jnp.where(even, last, first).astype(BF16)
+    outer_ref[...] = jnp.where(even, first, last).astype(BF16)
     for copy in copies[1:]:
         copy.wait()
 
 
 def stencil_kernel(
-    plan, state_ref, west_ref, east_ref, inner_ref, outer_ref, diff_ref, wind_ref, flags_ref, *refs
+    plan, state_ref, outer_ref, west_ref, east_ref, inner_ref, diff_ref, wind_ref, flags_ref, *refs
 ):
     refs = list(refs)
     even = band_place()
@@ -145,15 +145,16 @@
     columns = lons * lats
     kept = kept_ref.shape[1]
     row = iota((lats, levels), 0)
+    inner_rows, outer_rows = inner_ref[...].astype(F32), outer_ref[...].astype(F32)
     for number in range(variables):
         spread_by = diff_ref[number : number + 1, :]
         spot = plan.spot(number, variables)
         for lon in range(lons):
             center = state_ref[lon, number]
-            east = state_ref[lon + 1, number] if lon + 1 < lons else east_ref[number]
-            west = state_ref[lon - 1, number] if lon else west_ref[number]
-            inner = inner_ref[lon, number : number + 1, :]
-            outer = outer_ref[lon, number : number + 1, :]
+            east = state_ref[lon + 1, number] if lon + 1 < lons else east_ref[number].astype(F32)
+            west = state_ref[lon - 1, number] if lon else west_ref[number].astype(F32)
+            inner = inner_rows[lon, number : number + 1, :]
+            outer = outer_rows[lon, number : number + 1, :]
             north = jnp.where(
                 row == lats - 1,
                 jnp.where(even, inner, outer),
@@ -365,13 +366,13 @@
 
 def exchanged(state, *others):
     lons, variables, lats, levels = state.shape
-    lon_edge = shape((variables, lats, levels), F32)
-    lat_edge = shape((lons, variables, levels), F32)
+    lon_edge = shape((variables, lats, levels), BF16)
+    lat_edge = shape((lons, variables, levels), BF16)
     values = (state,) + others
-    *values, top, bottom, inner, outer = call(
+    *values, outer, top, bottom, inner = call(
         edge_kernel,
         [HB] * len(values),
-        [shape(v.shape, v.dtype) for v in values] + [lon_edge, lon_edge, lat_edge, lat_edge],
+        [shape(v.shape, v.dtype) for v in values] + [lat_edge, lon_edge, lon_edge, lat_edge],
         [pltpu.SemaphoreType.DMA((len(values),))],
     )(*[far(v) for v in values])
     tiles = lax.axis_size("tile")
@@ -386,7 +387,7 @@
     west = lax.ppermute(top, "tile", up)
     east = lax.ppermute(bottom, "tile", [(b, a) for a, b in up])
     inner = swap(inner, 0)
-    return values, (west, east, inner, outer)
+    return values, (outer, west, east, inner)
 
 
 def body(

time: 66.9 us -> 64.2 us (0.960)
  blocking collectives: 48.4 us -> 45.1 us
  starting transfers between devices: 5.87 us -> 8.93 us
  waiting for transfers between devices: 2.51 us -> 0.01 us
    all_to_all x1, blocking collectives: 34.2 us -> 30.9 us  [body(): rows = lax.all_to_all(rows, axes, split_axis=0, concat_axis=0, tiled=True)]
    ppermute x2, starting transfers between devices: 0.66 us -> 3.72 us  [swap(): lax.ppermute(values, ('lat', 'emu'), pairs + [(b, a) for a, b in pairs])]
    ppermute x1, waiting for transfers between devices: 1.61 us -> 0.01 us  [exchanged(): west = lax.ppermute(top, 'tile', up)]
    ppermute x1, waiting for transfers between devices: 0.9 us -> 0.01 us  [exchanged(): east = lax.ppermute(bottom, 'tile', [(b, a) for a, b in up])]
  transfers between devices with their start and end apart: 4 -> 4, of which waited for: 2 -> 0; matrix products, arithmetic and copies ran while one was open for 0% -> 0% of each run, Pallas kernels for 1% -> 1%
where the time goes in v4:
time: 64.2 us; the launch traced here: 64 us
  blocking collectives  45.1 us (70%)
  Pallas kernels  9.21 us (14%)
  starting transfers between devices  8.93 us (14%)
  between operations  0.74 us (1%)
    all_to_all x1, blocking collectives, body(): rows = lax.all_to_all(rows, axes, split_axis=0, concat_axis=0, tiled=True)  30.9 us
    all_to_all x1, blocking collectives, body(): made = lax.all_to_all(made, axes, split_axis=0, concat_axis=0, tiled=True)  14.2 us
    pallas_call x1, Pallas kernels, body(): call(functools.partial(network_kernel, plan), [VM] * 5 + [HB] * 2, shape(...  4.37 us
    ppermute x2, starting transfers between devices, swap(): lax.ppermute(values, ('lat', 'emu'), pairs + [(b, a) for a, b in pairs])  3.72 us
    ppermute x1, starting transfers between devices, exchanged(): west = lax.ppermute(top, 'tile', up)  3.12 us
    ppermute x1, starting transfers between devices, exchanged(): east = lax.ppermute(bottom, 'tile', [(b, a) for a, b in up])  2.09 us
    pallas_call x1, Pallas kernels, exchanged(): call(edge_kernel, [HB] * len(values), [shape(v.shape, v.dtype) for v in v...  1.87 us
    pallas_call x1, Pallas kernels, body(): call(functools.partial(stencil_kernel, plan), [VM] * (8 + len(packs)), [s...  1.43 us
  transfers between devices with their start and end apart: 4, of which 0 were waited for; matrix products, arithmetic and copies ran while one was open for 0% of the time, Pallas kernels for 1%

profile of v4, /device:TPU:0, one launch (start us, length us, event | category | flops | bytes accessed | tf_op | source)
XLA Modules:
  0.0 64.0 jit_solution(6160176023121052640)
XLA Ops:
  0.0 0.0 copy-start.1
  0.0 0.0 copy-start.3
  0.0 0.0 copy-start.2
  0.0 0.0 copy-start
  0.0 1.9 %shard_map.118 = (f32[16,12,16,128]{3,2,1,0:T(8,128)S(1)}, f32[12,128]{1,0:T(8,128)S(1)}, f32[16,16]{1,0:T(8,128)S(1)}, s32[16,16]{1,0:T(8,128)S(1)}, s32[1,256]...) custom-call(f32[16,12,16,128]{3,2,1,0:T(8,128)} %bitcast.12, ...), custom_call_target="tpu_custom_call" | custom-call | tf_op jit(solution)/shard_map/pallas_call | solution.py:372
  1.9 3.1 %collective-permute-start.1 = (bf16[12,16,128]{2,1,0:T(8,128)(2,1)S(1)}, bf16[12,16,128]{2,1,0:T(8,128)(2,1)S(1)}, u32[]{:S(2)}, u32[]{:S(2)}) collective-permute-start(bf16[12,16,128]{2,1,0:T(8,128)(2,1)S(1)} %get-tuple-element.24), channel_id=1, source_target_pairs={{0,8},{8,16},{16,24},{24,0},{1,9},{9,17},{17,25},{25,1},{2,10},{10... | collective-permute-start | bytes 147464 | tf_op jit(solution)/shard_map/ppermute | solution.py:387
  5.0 2.1 %collective-permute-start.2 = (bf16[12,16,128]{2,1,0:T(8,128)(2,1)S(1)}, bf16[12,16,128]{2,1,0:T(8,128)(2,1)S(1)}, u32[]{:S(2)}, u32[]{:S(2)}) collective-permute-start(bf16[12,16,128]{2,1,0:T(8,128)(2,1)S(1)} %get-tuple-element.25), channel_id=1, source_target_pairs={{8,0},{16,8},{24,16},{0,24},{9,1},{17,9},{25,17},{1,25},{10,2},{18... | collective-permute-start | bytes 147464 | tf_op jit(solution)/shard_map/ppermute | solution.py:388
  7.1 0.7 %collective-permute-start = (bf16[16,12,128]{2,1,0:T(8,128)(2,1)S(1)}, bf16[16,12,128]{2,1,0:T(8,128)(2,1)S(1)}, u32[]{:S(2)}, u32[]{:S(2)}) collective-permute-start(bf16[16,12,128]{2,1,0:T(8,128)(2,1)S(1)} %get-tuple-element.23), channel_id=1, source_target_pairs={{1,2},{3,4},{5,6},{2,1},{4,3},{6,5},{9,10},{11,12},{13,14},{10,9},... | collective-permute-start | bytes 147464 | tf_op jit(solution)/shard_map/ppermute | solution.py:384
  7.8 3.1 %collective-permute-start.3 = (bf16[16,12,128]{2,1,0:T(8,128)(2,1)S(1)}, bf16[16,12,128]{2,1,0:T(8,128)(2,1)S(1)}, u32[]{:S(2)}, u32[]{:S(2)}) collective-permute-start(bf16[16,12,128]{2,1,0:T(8,128)(2,1)S(1)} %get-tuple-element.26), channel_id=1, source_target_pairs={{0,1},{2,3},{4,5},{6,7},{1,0},{3,2},{5,4},{7,6},{8,9},{10,11},{12,... | collective-permute-start | bytes 147464 | tf_op jit(solution)/shard_map/ppermute | solution.py:384
  11.5 0.4 shard_map.119
  11.9 0.0 collective-permute-done.1.west_ref
  11.9 0.0 collective-permute-done.2.east_ref
  12.0 0.0 collective-permute-done.outer_ref
  12.0 0.0 collective-permute-done.3.inner_ref
  12.0 1.4 %shard_map.120 = (bf16[16,248,128]{2,1,0:T(8,128)(2,1)S(1)}, f32[16,4,16,128]{3,2,1,0:T(8,128)S(1)}) custom-call(f32[16,12,16,128]{3,2,1,0:T(8,128)S(1)} %get-tuple-element.22.state_ref, bf16[16,12,128]{2,1,0:T(8,128)(2,1)S(1)} %collective-permute-done.outer_ref, bf16[12,16,128]{2,1,0:T(8,128)(2,1)S(1)} %collective-permute-done.1.west_ref, ...), custom_call_target="tpu_custom_call" | custom-call | tf_op jit(solution)/shard_map/pallas_call | solution.py:426
  13.4 30.9 %all_to_all.10.rows_ref = bf16[16,248,128]{2,1,0:T(8,128)(2,1)S(1)} all-to-all(bf16[16,248,128]{2,1,0:T(8,128)(2,1)S(1)} %get-tuple-element.35), channel_id=1, replica_groups=mesh['tile'=4,'lat'=4,'emu'=2] {'tile','lat'}, dimensions={0} | all-to-all | bytes 2031616 | tf_op jit(solution)/shard_map/all_to_all | solution.py:437
  44.4 0.0 copy-done.1
  44.4 0.0 copy-done.3
  44.4 0.0 copy-done.2
  44.4 0.0 copy-done
  44.4 4.4 %shard_map.121 = bf16[16,80,128]{2,1,0:T(8,128)(2,1)S(1)} custom-call(bf16[16,248,128]{2,1,0:T(8,128)(2,1)S(1)} %all_to_all.10.rows_ref, f32[1,1024]{1,0:T(1,128)S(1)} %copy-done.2, f32[1,1024]{1,0:T(1,128)S(1)} %copy-done.3, f32[2,1024]{1,0:T(2,128)S(1)} %bitcast.10, bf16[1536,1024]{1,0:T(8,128)(2,1)S(1)} %bitcast.9, bf16[2,1024,1024]{2,1,0:T(8,128)(2,1)} %bitcast.11, ...), custom_call_target="tpu_custom_call" | custom-call | tf_op jit(solution)/shard_map/pallas_call | solution.py:438
  48.8 14.2 %all_to_all.11.rows_ref = bf16[16,80,128]{2,1,0:T(8,128)(2,1)S(1)} all-to-all(bf16[16,80,128]{2,1,0:T(8,128)(2,1)S(1)} %shard_map.121), channel_id=1, replica_groups=mesh['tile'=4,'lat'=4,'emu'=2] {'tile','lat'}, dimensions={0} | all-to-all | bytes 655360 | tf_op jit(solution)/shard_map/all_to_all | solution.py:450
  62.9 1.1 %shard_map.122 = f32[1024,128]{1,0:T(8,128)} custom-call(bf16[16,80,128]{2,1,0:T(8,128)(2,1)S(1)} %all_to_all.11.rows_ref, f32[16,4,16,128]{3,2,1,0:T(8,128)S(1)} %get-tuple-element.36.kept_ref, bf16[256,256]{1,0:T(8,128)(2,1)S(1)} %get-tuple-element.37.refs_0_, bf16[256,256]{1,0:T(8,128)(2,1)S(1)} %get-tuple-element.38.refs_1_), custom_call_target="tpu_custom_call" | custom-call | tf_op jit(solution)/shard_map/pallas_call | solution.py:451
Async XLA Ops:
  0.0 44.4 %copy-start.1 = (f32[1,2,1024]{2,1,0:T(2,128)S(1)}, f32[1,2,1024]{2,1,0:T(2,128)}, u32[]{:S(2)}) copy-start(f32[1,2,1024]{2,1,0:T(2,128)} %param.22) | copy-start | bytes 24580
  0.0 44.4 %copy-start.3 = (f32[1,1024]{1,0:T(1,128)S(1)}, f32[1,1024]{1,0:T(1,128)}, u32[]{:S(2)}) copy-start(f32[1,1024]{1,0:T(1,128)} %land_add.1) | copy-start | bytes 12292
  0.0 44.4 %copy-start.2 = (f32[1,1024]{1,0:T(1,128)S(1)}, f32[1,1024]{1,0:T(1,128)}, u32[]{:S(2)}) copy-start(f32[1,1024]{1,0:T(1,128)} %b_first.1) | copy-start | bytes 12292
  0.0 44.4 %copy-start = (bf16[1,1536,1024]{2,1,0:T(8,128)(2,1)S(1)}, bf16[1,1536,1024]{2,1,0:T(8,128)(2,1)}, u32[]{:S(2)}) copy-start(bf16[1,1536,1024]{2,1,0:T(8,128)(2,1)} %param.18) | copy-start | bytes 9437188
  1.9 10.0 %collective-permute-start.1 = (bf16[12,16,128]{2,1,0:T(8,128)(2,1)S(1)}, bf16[12,16,128]{2,1,0:T(8,128)(2,1)S(1)}, u32[]{:S(2)}, u32[]{:S(2)}) collective-permute-start(bf16[12,16,128]{2,1,0:T(8,128)(2,1)S(1)} %get-tuple-element.24), channel_id=1, source_target_pairs={{0,8},{8,16},{16,24},{24,0},{1,9},{9,17},{17,25},{25,1},{2,10},{10... | collective-permute-start | bytes 147464 | tf_op jit(solution)/shard_map/ppermute | solution.py:387
  5.0 6.9 %collective-permute-start.2 = (bf16[12,16,128]{2,1,0:T(8,128)(2,1)S(1)}, bf16[12,16,128]{2,1,0:T(8,128)(2,1)S(1)}, u32[]{:S(2)}, u32[]{:S(2)}) collective-permute-start(bf16[12,16,128]{2,1,0:T(8,128)(2,1)S(1)} %get-tuple-element.25), channel_id=1, source_target_pairs={{8,0},{16,8},{24,16},{0,24},{9,1},{17,9},{25,17},{1,25},{10,2},{18... | collective-permute-start | bytes 147464 | tf_op jit(solution)/shard_map/ppermute | solution.py:388
  7.1 4.9 %collective-permute-start = (bf16[16,12,128]{2,1,0:T(8,128)(2,1)S(1)}, bf16[16,12,128]{2,1,0:T(8,128)(2,1)S(1)}, u32[]{:S(2)}, u32[]{:S(2)}) collective-permute-start(bf16[16,12,128]{2,1,0:T(8,128)(2,1)S(1)} %get-tuple-element.23), channel_id=1, source_target_pairs={{1,2},{3,4},{5,6},{2,1},{4,3},{6,5},{9,10},{11,12},{13,14},{10,9},... | collective-permute-start | bytes 147464 | tf_op jit(solution)/shard_map/ppermute | solution.py:384
  7.8 4.2 %collective-permute-start.3 = (bf16[16,12,128]{2,1,0:T(8,128)(2,1)S(1)}, bf16[16,12,128]{2,1,0:T(8,128)(2,1)S(1)}, u32[]{:S(2)}, u32[]{:S(2)}) collective-permute-start(bf16[16,12,128]{2,1,0:T(8,128)(2,1)S(1)} %get-tuple-element.26), channel_id=1, source_target_pairs={{0,1},{2,3},{4,5},{6,7},{1,0},{3,2},{5,4},{7,6},{8,9},{10,11},{12,... | collective-permute-start | bytes 147464 | tf_op jit(solution)/shard_map/ppermute | solution.py:384

commit v5 on v4

--- a/solution.py
+++ b/solution.py
@@ -48,11 +48,14 @@
     return row + source * (plan.chunk - plan.rest) + place * plan.rest, iota((small, large), 1)
 
 
-def route_kernel(plan, count_ref, routes_ref, land_ref, wind_ref, *refs):
+def route_kernel(plan, count_ref, routes_ref, land_ref, wind_ref, first_hbm, *refs):
     refs = list(refs)
+    sem, column_ref, w_part = refs.pop(), refs.pop(), refs.pop()
+    total = first_hbm.shape[0]
+    copy = pltpu.make_async_copy(first_hbm.at[total - w_part.shape[0] :], w_part, sem)
+    copy.start()
     flags_ref, wind_out = refs[:2]
     refs = refs[2:]
-    column_ref = refs.pop()
     experts = plan.experts
     columns = routes_ref.shape[1]
     lons, lats = land_ref.shape
@@ -104,6 +107,7 @@
     at = upright(rank).astype(jnp.int32) == iota((columns, lanes), 1)
     marked = jnp.where(at, column_ref[...], 0.0).astype(BF16)
     flags_ref[...] = jnp.dot(owner_hot, marked, preferred_element_type=F32)
+    copy.wait()
 
 
 def band_place():
@@ -115,7 +119,7 @@
     *refs, outer_ref, top_ref, bottom_ref, inner_ref, sems = refs
     half = len(refs) // 2
     copies = [
-        pltpu.make_async_copy(source, target, sems.at[k])
+        pltpu.make_async_copy(source.at[: target.shape[0]], target, sems.at[k])
         for k, (source, target) in enumerate(zip(refs[:half], refs[half:]))
     ]
     for copy in copies:
@@ -207,26 +211,16 @@
     b_first,
     land_add,
     b_inner,
-    w_first,
-    inner_hbm,
-    last_hbm,
+    w_head,
+    w_tail,
+    w_inner,
+    w_last,
     out_ref,
     x_ref,
-    w_inner,
-    w_last,
-    sems,
 ):
     sources, _, levels = rows_ref.shape
-    pairs = [(inner_hbm.at[k], w_inner.at[k]) for k in range(w_inner.shape[0])]
-    pairs += [(last_hbm, w_last)]
-    copies = [
-        pltpu.make_async_copy(source, target, sems.at[k])
-        for k, (source, target) in enumerate(pairs)
-    ]
-    for copy in copies:
-        copy.start()
-    copies.reverse()
-    variables = w_first.shape[0] // levels
+    step = w_head.shape[0]
+    variables = (step + w_tail.shape[0]) // levels
     lead = sources * plan.full
     small = sources * plan.rest
     marks = rows_ref[:, plan.rows(variables) :, :].astype(F32)
@@ -263,13 +257,12 @@
         target, column = spread(plan, 0)
         flags.append(jnp.dot(hot(target == column), tall, preferred_element_type=F32)[:, :1])
     flag = jnp.concatenate(flags, axis=0)
-    pre = jnp.dot(x_ref[...], w_first[...], preferred_element_type=F32) + b_first[...]
+    pre = jnp.dot(x_ref[:, :step], w_head[...], preferred_element_type=F32) + b_first[...]
+    pre += jnp.dot(x_ref[:, step:], w_tail[...], preferred_element_type=F32)
     hidden = jax.nn.silu(pre + flag * land_add[...]).astype(BF16)
     for number in range(w_inner.shape[0]):
-        copies.pop().wait()
         pre = jnp.dot(hidden, w_inner[number], preferred_element_type=F32)
         hidden = jax.nn.silu(pre + b_inner[number : number + 1, :]).astype(BF16)
-    copies.pop().wait()
     made = jnp.dot(hidden, w_last[...], preferred_element_type=F32).astype(BF16)
     outs = made.shape[1] // levels
     if plan.full:
@@ -364,7 +357,7 @@
     return pltpu.with_memory_space_constraint(values, pltpu.HBM)
 
 
-def exchanged(state, *others):
+def exchanged(head, state, *others):
     lons, variables, lats, levels = state.shape
     lon_edge = shape((variables, lats, levels), BF16)
     lat_edge = shape((lons, variables, levels), BF16)
@@ -372,7 +365,9 @@
     *values, outer, top, bottom, inner = call(
         edge_kernel,
         [HB] * len(values),
-        [shape(v.shape, v.dtype) for v in values] + [lat_edge, lon_edge, lon_edge, lat_edge],
+        [shape(v.shape, v.dtype) for v in values[:-1]]
+        + [shape((head, values[-1].shape[1]), BF16)]
+        + [lat_edge, lon_edge, lon_edge, lat_edge],
         [pltpu.SemaphoreType.DMA((len(values),))],
     )(*[far(v) for v in values])
     tiles = lax.axis_size("tile")
@@ -400,8 +395,19 @@
     capacity = max(2, columns * 5 // (4 * experts))
     plan = Plan(experts, capacity)
     state = jnp.transpose(state, (0, 2, 1, 3))
-    (state, diffusivity, wind, land_mask, routes), halos = exchanged(
-        state, diffusivity, wind, land_mask, routes.reshape(1, columns)
+    w_in = far(w_in[0])
+    head = w_in.shape[0] // 2
+    (state, diffusivity, wind, land_mask, routes, b_in, land_vec, b_hid, w_head), halos = exchanged(
+        head,
+        state,
+        diffusivity,
+        wind,
+        land_mask,
+        routes.reshape(1, columns),
+        b_in,
+        land_vec,
+        b_hid[0],
+        w_in,
     )
 
     shapes = [shape((experts, levels), F32), shape((columns, levels), F32)]
@@ -416,12 +422,12 @@
         ]
     made = call(
         functools.partial(route_kernel, plan),
-        [SM, VM, VM, VM],
-        shapes,
-        [pltpu.VMEM((columns, levels), F32)],
-    )(counts.reshape(1, 1), routes, land_mask, wind)
-    flags, half_wind = made[:2]
-    packs, picks = made[2::2], made[3::2]
+        [SM, VM, VM, VM, HB],
+        shapes + [shape((w_in.shape[0] - head, w_in.shape[1]), BF16)],
+        [pltpu.VMEM((columns, levels), F32), pltpu.SemaphoreType.DMA],
+    )(counts.reshape(1, 1), routes, land_mask, wind, w_in)
+    flags, half_wind, *made, w_tail = made
+    packs, picks = made[::2], made[1::2]
 
     rows, kept = call(
         functools.partial(stencil_kernel, plan),
@@ -437,16 +443,13 @@
     rows = lax.all_to_all(rows, axes, split_axis=0, concat_axis=0, tiled=True)
     made = call(
         functools.partial(network_kernel, plan),
-        [VM] * 5 + [HB] * 2,
+        [VM] * 8,
         shape((experts, plan.rows(outs), levels), BF16),
         [
             pltpu.VMEM((experts * capacity, variables * levels), BF16),
-            pltpu.VMEM(w_hid.shape[1:], BF16),
-            pltpu.VMEM(w_out.shape[1:], BF16),
-            pltpu.SemaphoreType.DMA((w_hid.shape[1] + 1,)),
         ],
-        32,
-    )(rows, b_in, land_vec, b_hid[0], w_in[0], far(w_hid[0]), far(w_out[0]))
+        16,
+    )(rows, b_in, land_vec, b_hid, w_head, w_tail, w_hid[0], w_out[0])
     made = lax.all_to_all(made, axes, split_axis=0, concat_axis=0, tiled=True)
     out = call(
         functools.partial(finish_kernel, plan),

time: 64.2 us -> 63.2 us (0.984)
  blocking collectives: 45.1 us -> 44 us
    all_to_all x1, blocking collectives: 30.9 us -> 29.9 us  [body(): rows = lax.all_to_all(rows, axes, split_axis=0, concat_axis=0, tiled=True)]
  transfers between devices with their start and end apart: 4 -> 4, of which waited for: 0 -> 0; matrix products, arithmetic and copies ran while one was open for 0% -> 0% of each run, Pallas kernels for 1% -> 2%
where the time goes in v5:
time: 63.2 us; the launch traced here: 63 us
  blocking collectives  44 us (70%)
  Pallas kernels  9.3 us (15%)
  starting transfers between devices  8.92 us (14%)
  between operations  0.74 us (1%)
    all_to_all x1, blocking collectives, body(): rows = lax.all_to_all(rows, axes, split_axis=0, concat_axis=0, tiled=True)  29.9 us
    all_to_all x1, blocking collectives, body(): made = lax.all_to_all(made, axes, split_axis=0, concat_axis=0, tiled=True)  14.2 us
    ppermute x2, starting transfers between devices, swap(): lax.ppermute(values, ('lat', 'emu'), pairs + [(b, a) for a, b in pairs])  3.72 us
    pallas_call x1, Pallas kernels, body(): call(functools.partial(network_kernel, plan), [VM] * 8, shape((experts, p...  3.19 us
    ppermute x1, starting transfers between devices, exchanged(): west = lax.ppermute(top, 'tile', up)  3.1 us
    ppermute x1, starting transfers between devices, exchanged(): east = lax.ppermute(bottom, 'tile', [(b, a) for a, b in up])  2.09 us
    pallas_call x1, Pallas kernels, exchanged(): call(edge_kernel, [HB] * len(values), [shape(v.shape, v.dtype) for v in v...  2.07 us
    pallas_call x1, Pallas kernels, body(): call(functools.partial(route_kernel, plan), [SM, VM, VM, VM, HB], shapes...  1.51 us
  transfers between devices with their start and end apart: 4, of which 0 were waited for; matrix products, arithmetic and copies ran while one was open for 0% of the time, Pallas kernels for 2%

profile of v5, /device:TPU:0, one launch (start us, length us, event | category | flops | bytes accessed | tf_op | source)
XLA Modules:
  0.0 63.0 jit_solution(17294289607182657438)
XLA Ops:
  0.0 2.1 %shard_map.118 = (f32[16,12,16,128]{3,2,1,0:T(8,128)S(1)}, f32[12,128]{1,0:T(8,128)S(1)}, f32[16,16]{1,0:T(8,128)S(1)}, s32[16,16]{1,0:T(8,128)S(1)}, s32[1,256]...) custom-call(f32[16,12,16,128]{3,2,1,0:T(8,128)} %bitcast.13, ...), custom_call_target="tpu_custom_call" | custom-call | tf_op jit(solution)/shard_map/pallas_call | solution.py:365
  2.1 3.1 %collective-permute-start.1 = (bf16[12,16,128]{2,1,0:T(8,128)(2,1)S(1)}, bf16[12,16,128]{2,1,0:T(8,128)(2,1)S(1)}, u32[]{:S(2)}, u32[]{:S(2)}) collective-permute-start(bf16[12,16,128]{2,1,0:T(8,128)(2,1)S(1)} %get-tuple-element.29), channel_id=1, source_target_pairs={{0,8},{8,16},{16,24},{24,0},{1,9},{9,17},{17,25},{25,1},{2,10},{10... | collective-permute-start | bytes 147464 | tf_op jit(solution)/shard_map/ppermute | solution.py:382
  5.2 2.1 %collective-permute-start.2 = (bf16[12,16,128]{2,1,0:T(8,128)(2,1)S(1)}, bf16[12,16,128]{2,1,0:T(8,128)(2,1)S(1)}, u32[]{:S(2)}, u32[]{:S(2)}) collective-permute-start(bf16[12,16,128]{2,1,0:T(8,128)(2,1)S(1)} %get-tuple-element.30), channel_id=1, source_target_pairs={{8,0},{16,8},{24,16},{0,24},{9,1},{17,9},{25,17},{1,25},{10,2},{18... | collective-permute-start | bytes 147464 | tf_op jit(solution)/shard_map/ppermute | solution.py:383
  7.3 0.7 %collective-permute-start = (bf16[16,12,128]{2,1,0:T(8,128)(2,1)S(1)}, bf16[16,12,128]{2,1,0:T(8,128)(2,1)S(1)}, u32[]{:S(2)}, u32[]{:S(2)}) collective-permute-start(bf16[16,12,128]{2,1,0:T(8,128)(2,1)S(1)} %get-tuple-element.28), channel_id=1, source_target_pairs={{1,2},{3,4},{5,6},{2,1},{4,3},{6,5},{9,10},{11,12},{13,14},{10,9},... | collective-permute-start | bytes 147464 | tf_op jit(solution)/shard_map/ppermute | solution.py:379
  7.9 3.1 %collective-permute-start.3 = (bf16[16,12,128]{2,1,0:T(8,128)(2,1)S(1)}, bf16[16,12,128]{2,1,0:T(8,128)(2,1)S(1)}, u32[]{:S(2)}, u32[]{:S(2)}) collective-permute-start(bf16[16,12,128]{2,1,0:T(8,128)(2,1)S(1)} %get-tuple-element.31), channel_id=1, source_target_pairs={{0,1},{2,3},{4,5},{6,7},{1,0},{3,2},{5,4},{7,6},{8,9},{10,11},{12,... | collective-permute-start | bytes 147464 | tf_op jit(solution)/shard_map/ppermute | solution.py:379
  11.7 0.0 copy-start.1
  11.7 1.5 %shard_map.119 = (f32[16,128]{1,0:T(8,128)S(1)}, f32[256,128]{1,0:T(8,128)S(1)}, bf16[256,256]{1,0:T(8,128)(2,1)S(1)}, bf16[256,256]{1,0:T(8,128)(2,1)S(1)}, bf1...) custom-call(s32[1,1]{1,0:T(1,128)} %bitcast.8.count_ref, ...), custom_call_target="tpu_custom_call" | custom-call | tf_op jit(solution)/shard_map/pallas_call | solution.py:423
  13.2 0.0 collective-permute-done.1.west_ref
  13.2 0.0 collective-permute-done.2.east_ref
  13.2 0.0 collective-permute-done.outer_ref
  13.2 0.0 collective-permute-done.3.inner_ref
  13.2 0.0 copy-start
  13.2 1.4 %shard_map.120 = (bf16[16,248,128]{2,1,0:T(8,128)(2,1)S(1)}, f32[16,4,16,128]{3,2,1,0:T(8,128)S(1)}) custom-call(f32[16,12,16,128]{3,2,1,0:T(8,128)S(1)} %get-tuple-element.27.state_ref, bf16[16,12,128]{2,1,0:T(8,128)(2,1)S(1)} %collective-permute-done.outer_ref, bf16[12,16,128]{2,1,0:T(8,128)(2,1)S(1)} %collective-permute-done.1.west_ref, ...), custom_call_target="tpu_custom_call" | custom-call | tf_op jit(solution)/shard_map/pallas_call | solution.py:432
  14.7 29.9 %all_to_all.10.rows_ref = bf16[16,248,128]{2,1,0:T(8,128)(2,1)S(1)} all-to-all(bf16[16,248,128]{2,1,0:T(8,128)(2,1)S(1)} %get-tuple-element.40), channel_id=1, replica_groups=mesh['tile'=4,'lat'=4,'emu'=2] {'tile','lat'}, dimensions={0} | all-to-all | bytes 2031616 | tf_op jit(solution)/shard_map/all_to_all | solution.py:443
  44.5 0.0 copy-done.1
  44.5 0.0 copy-done
  44.5 3.2 %shard_map.121 = bf16[16,80,128]{2,1,0:T(8,128)(2,1)S(1)} custom-call(bf16[16,248,128]{2,1,0:T(8,128)(2,1)S(1)} %all_to_all.10.rows_ref, f32[1,1024]{1,0:T(1,128)S(1)} %get-tuple-element.41.b_first, f32[1,1024]{1,0:T(1,128)S(1)} %get-tuple-element.42.land_add, f32[2,1024]{1,0:T(2,128)S(1)} %get-tuple-element.43.b_inner, ...), custom_call_target="tpu_custom_call" | custom-call | tf_op jit(solution)/shard_map/pallas_call | solution.py:444
  47.7 14.2 %all_to_all.11.rows_ref = bf16[16,80,128]{2,1,0:T(8,128)(2,1)S(1)} all-to-all(bf16[16,80,128]{2,1,0:T(8,128)(2,1)S(1)} %shard_map.121), channel_id=1, replica_groups=mesh['tile'=4,'lat'=4,'emu'=2] {'tile','lat'}, dimensions={0} | all-to-all | bytes 655360 | tf_op jit(solution)/shard_map/all_to_all | solution.py:453
  61.9 1.1 %shard_map.122 = f32[1024,128]{1,0:T(8,128)} custom-call(bf16[16,80,128]{2,1,0:T(8,128)(2,1)S(1)} %all_to_all.11.rows_ref, f32[16,4,16,128]{3,2,1,0:T(8,128)S(1)} %get-tuple-element.46.kept_ref, bf16[256,256]{1,0:T(8,128)(2,1)S(1)} %get-tuple-element.47.refs_0_, bf16[256,256]{1,0:T(8,128)(2,1)S(1)} %get-tuple-element.48.refs_1_), custom_call_target="tpu_custom_call" | custom-call | tf_op jit(solution)/shard_map/pallas_call | solution.py:454
Async XLA Ops:
  2.1 11.1 %collective-permute-start.1 = (bf16[12,16,128]{2,1,0:T(8,128)(2,1)S(1)}, bf16[12,16,128]{2,1,0:T(8,128)(2,1)S(1)}, u32[]{:S(2)}, u32[]{:S(2)}) collective-permute-start(bf16[12,16,128]{2,1,0:T(8,128)(2,1)S(1)} %get-tuple-element.29), channel_id=1, source_target_pairs={{0,8},{8,16},{16,24},{24,0},{1,9},{9,17},{17,25},{25,1},{2,10},{10... | collective-permute-start | bytes 147464 | tf_op jit(solution)/shard_map/ppermute | solution.py:382
  5.2 8.0 %collective-permute-start.2 = (bf16[12,16,128]{2,1,0:T(8,128)(2,1)S(1)}, bf16[12,16,128]{2,1,0:T(8,128)(2,1)S(1)}, u32[]{:S(2)}, u32[]{:S(2)}) collective-permute-start(bf16[12,16,128]{2,1,0:T(8,128)(2,1)S(1)} %get-tuple-element.30), channel_id=1, source_target_pairs={{8,0},{16,8},{24,16},{0,24},{9,1},{17,9},{25,17},{1,25},{10,2},{18... | collective-permute-start | bytes 147464 | tf_op jit(solution)/shard_map/ppermute | solution.py:383
  7.3 5.9 %collective-permute-start = (bf16[16,12,128]{2,1,0:T(8,128)(2,1)S(1)}, bf16[16,12,128]{2,1,0:T(8,128)(2,1)S(1)}, u32[]{:S(2)}, u32[]{:S(2)}) collective-permute-start(bf16[16,12,128]{2,1,0:T(8,128)(2,1)S(1)} %get-tuple-element.28), channel_id=1, source_target_pairs={{1,2},{3,4},{5,6},{2,1},{4,3},{6,5},{9,10},{11,12},{13,14},{10,9},... | collective-permute-start | bytes 147464 | tf_op jit(solution)/shard_map/ppermute | solution.py:379
  7.9 5.3 %collective-permute-start.3 = (bf16[16,12,128]{2,1,0:T(8,128)(2,1)S(1)}, bf16[16,12,128]{2,1,0:T(8,128)(2,1)S(1)}, u32[]{:S(2)}, u32[]{:S(2)}) collective-permute-start(bf16[16,12,128]{2,1,0:T(8,128)(2,1)S(1)} %get-tuple-element.31), channel_id=1, source_target_pairs={{0,1},{2,3},{4,5},{6,7},{1,0},{3,2},{5,4},{7,6},{8,9},{10,11},{12,... | collective-permute-start | bytes 147464 | tf_op jit(solution)/shard_map/ppermute | solution.py:379
  11.7 32.9 %copy-start.1 = (bf16[1,1024,512]{2,1,0:T(8,128)(2,1)S(1)}, bf16[1,1024,512]{2,1,0:T(8,128)(2,1)}, u32[]{:S(2)}) copy-start(bf16[1,1024,512]{2,1,0:T(8,128)(2,1)} %param.23) | copy-start | bytes 3145732
  13.2 31.3 %copy-start = (bf16[1,2,1024,1024]{3,2,1,0:T(8,128)(2,1)S(1)}, bf16[1,2,1024,1024]{3,2,1,0:T(8,128)(2,1)}, u32[]{:S(2)}) copy-start(bf16[1,2,1024,1024]{3,2,1,0:T(8,128)(2,1)} %param.21) | copy-start | bytes 12582916

commit v6 on v5

--- a/solution.py
+++ b/solution.py
@@ -48,9 +48,27 @@
     return row + source * (plan.chunk - plan.rest) + place * plan.rest, iota((small, large), 1)
 
 
-def route_kernel(plan, count_ref, routes_ref, land_ref, wind_ref, first_hbm, *refs):
+def inside_stencil(state_ref, diff_ref, wind_ref, inside_ref):
+    lons, variables, lats, levels = state_ref.shape
+    row = iota((lats, levels), 0)
+    for number in range(variables):
+        spread_by = diff_ref[number : number + 1, :]
+        for lon in range(lons):
+            center = state_ref[lon, number]
+            east = state_ref[lon + 1, number] if lon + 1 < lons else jnp.zeros_like(center)
+            west = state_ref[lon - 1, number] if lon else jnp.zeros_like(center)
+            north = jnp.where(row == lats - 1, 0.0, pltpu.roll(center, lats - 1, 0))
+            south = jnp.where(row == 0, 0.0, pltpu.roll(center, 1, 0))
+            total = east + west + north + south - 4.0 * center
+            half = wind_ref[lon * lats : (lon + 1) * lats, :]
+            inside_ref[lon, number] = center + spread_by * total - half * (east - west)
+
+
+def route_kernel(
+    plan, count_ref, routes_ref, land_ref, wind_ref, state_ref, diff_ref, first_hbm, *refs
+):
     refs = list(refs)
-    sem, column_ref, w_part = refs.pop(), refs.pop(), refs.pop()
+    sem, column_ref, w_part, inside_ref = refs.pop(), refs.pop(), refs.pop(), refs.pop()
     total = first_hbm.shape[0]
     copy = pltpu.make_async_copy(first_hbm.at[total - w_part.shape[0] :], w_part, sem)
     copy.start()
@@ -107,6 +125,7 @@
     at = upright(rank).astype(jnp.int32) == iota((columns, lanes), 1)
     marked = jnp.where(at, column_ref[...], 0.0).astype(BF16)
     flags_ref[...] = jnp.dot(owner_hot, marked, preferred_element_type=F32)
+    inside_stencil(state_ref, diff_ref, wind_out, inside_ref)
     copy.wait()
 
 
@@ -138,38 +157,32 @@
 
 
 def stencil_kernel(
-    plan, state_ref, outer_ref, west_ref, east_ref, inner_ref, diff_ref, wind_ref, flags_ref, *refs
+    plan, inside_ref, outer_ref, west_ref, east_ref, inner_ref, diff_ref, wind_ref, flags_ref, *refs
 ):
     refs = list(refs)
     even = band_place()
     pack_full = refs.pop(0) if plan.full else None
     pack_rest = refs.pop(0) if plan.rest else None
     out_ref, kept_ref, feature_ref = refs
-    lons, variables, lats, levels = state_ref.shape
+    lons, variables, lats, levels = inside_ref.shape
     columns = lons * lats
     kept = kept_ref.shape[1]
     row = iota((lats, levels), 0)
-    inner_rows, outer_rows = inner_ref[...].astype(F32), outer_ref[...].astype(F32)
+    inner, outer = inner_ref[...].astype(F32), outer_ref[...].astype(F32)
+    north = jnp.where(even, inner, outer) * diff_ref[...]
+    south = jnp.where(even, outer, inner) * diff_ref[...]
     for number in range(variables):
         spread_by = diff_ref[number : number + 1, :]
         spot = plan.spot(number, variables)
         for lon in range(lons):
-            center = state_ref[lon, number]
-            east = state_ref[lon + 1, number] if lon + 1 < lons else east_ref[number].astype(F32)
-            west = state_ref[lon - 1, number] if lon else west_ref[number].astype(F32)
-            inner = inner_rows[lon, number : number + 1, :]
-            outer = outer_rows[lon, number : number + 1, :]
-            north = jnp.where(
-                row == lats - 1,
-                jnp.where(even, inner, outer),
-                pltpu.roll(center, lats - 1, 0),
-            )
-            south = jnp.where(
-                row == 0, jnp.where(even, outer, inner), pltpu.roll(center, 1, 0)
-            )
-            total = east + west + north + south - 4.0 * center
+            above = jnp.where(row == lats - 1, north[lon, number : number + 1, :], 0.0)
+            below = jnp.where(row == 0, south[lon, number : number + 1, :], above)
+            moved = inside_ref[lon, number] + below
             half = wind_ref[lon * lats : (lon + 1) * lats, :]
-            moved = center + spread_by * total - half * (east - west)
+            if lon == 0:
+                moved += (spread_by + half) * west_ref[number].astype(F32)
+            if lon == lons - 1:
+                moved += (spread_by - half) * east_ref[number].astype(F32)
             if number < kept:
                 kept_ref[lon, number] = moved
             feature_ref[lon * lats : (lon + 1) * lats, spot * levels : (spot + 1) * levels] = (
@@ -422,11 +435,11 @@
         ]
     made = call(
         functools.partial(route_kernel, plan),
-        [SM, VM, VM, VM, HB],
-        shapes + [shape((w_in.shape[0] - head, w_in.shape[1]), BF16)],
+        [SM, VM, VM, VM, VM, VM, HB],
+        shapes + [shape(state.shape, F32), shape((w_in.shape[0] - head, w_in.shape[1]), BF16)],
         [pltpu.VMEM((columns, levels), F32), pltpu.SemaphoreType.DMA],
-    )(counts.reshape(1, 1), routes, land_mask, wind, w_in)
-    flags, half_wind, *made, w_tail = made
+    )(counts.reshape(1, 1), routes, land_mask, wind, state, diffusivity, w_in)
+    flags, half_wind, *made, inside, w_tail = made
     packs, picks = made[::2], made[1::2]
 
     rows, kept = call(
@@ -437,7 +450,7 @@
             shape((lons, outs, lats, levels), F32),
         ],
         [pltpu.VMEM((columns, variables * levels), BF16)],
-    )(state, *halos, diffusivity, half_wind, flags, *packs)
+    )(inside, *halos, diffusivity, half_wind, flags, *packs)
 
     axes = ("tile", "lat")
     rows = lax.all_to_all(rows, axes, split_axis=0, concat_axis=0, tiled=True)

time: 63.2 us -> 62.7 us (level)
  Pallas kernels: 9.3 us -> 8.62 us
    pallas_call x1, Pallas kernels: 1.43 us -> 0.73 us  [body(): call(functools.partial(stencil_kernel, plan), [VM] * (8 + len(packs)), [s...]
where the time goes in v6:
time: 62.7 us; the launch traced here: 62.5 us
  blocking collectives  44.2 us (70%)
  starting transfers between devices  8.92 us (14%)
  Pallas kernels  8.62 us (14%)
  between operations  0.74 us (1%)
    all_to_all x1, blocking collectives, body(): rows = lax.all_to_all(rows, axes, split_axis=0, concat_axis=0, tiled=True)  30 us
    all_to_all x1, blocking collectives, body(): made = lax.all_to_all(made, axes, split_axis=0, concat_axis=0, tiled=True)  14.2 us
    ppermute x2, starting transfers between devices, swap(): lax.ppermute(values, ('lat', 'emu'), pairs + [(b, a) for a, b in pairs])  3.72 us
    pallas_call x1, Pallas kernels, body(): call(functools.partial(network_kernel, plan), [VM] * 8, shape((experts, p...  3.19 us
    ppermute x1, starting transfers between devices, exchanged(): west = lax.ppermute(top, 'tile', up)  3.1 us
    ppermute x1, starting transfers between devices, exchanged(): east = lax.ppermute(bottom, 'tile', [(b, a) for a, b in up])  2.09 us
    pallas_call x1, Pallas kernels, exchanged(): call(edge_kernel, [HB] * len(values), [shape(v.shape, v.dtype) for v in v...  2.07 us
    pallas_call x1, Pallas kernels, body(): call(functools.partial(route_kernel, plan), [SM, VM, VM, VM, VM, VM, HB],...  1.52 us
  transfers between devices with their start and end apart: 4, of which 0 were waited for; matrix products, arithmetic and copies ran while one was open for 0% of the time, Pallas kernels for 2%

profile of v6, /device:TPU:0, one launch (start us, length us, event | category | flops | bytes accessed | tf_op | source)
XLA Modules:
  0.0 62.5 jit_solution(9136614929129260174)
XLA Ops:
  0.0 2.1 %shard_map.118 = (f32[16,12,16,128]{3,2,1,0:T(8,128)S(1)}, f32[12,128]{1,0:T(8,128)S(1)}, f32[16,16]{1,0:T(8,128)S(1)}, s32[16,16]{1,0:T(8,128)S(1)}, s32[1,256]...) custom-call(f32[16,12,16,128]{3,2,1,0:T(8,128)} %bitcast.13, ...), custom_call_target="tpu_custom_call" | custom-call | tf_op jit(solution)/shard_map/pallas_call | solution.py:378
  2.1 3.1 %collective-permute-start.1 = (bf16[12,16,128]{2,1,0:T(8,128)(2,1)S(1)}, bf16[12,16,128]{2,1,0:T(8,128)(2,1)S(1)}, u32[]{:S(2)}, u32[]{:S(2)}) collective-permute-start(bf16[12,16,128]{2,1,0:T(8,128)(2,1)S(1)} %get-tuple-element.35), channel_id=1, source_target_pairs={{0,8},{8,16},{16,24},{24,0},{1,9},{9,17},{17,25},{25,1},{2,10},{10... | collective-permute-start | bytes 147464 | tf_op jit(solution)/shard_map/ppermute | solution.py:395
  5.2 2.1 %collective-permute-start.2 = (bf16[12,16,128]{2,1,0:T(8,128)(2,1)S(1)}, bf16[12,16,128]{2,1,0:T(8,128)(2,1)S(1)}, u32[]{:S(2)}, u32[]{:S(2)}) collective-permute-start(bf16[12,16,128]{2,1,0:T(8,128)(2,1)S(1)} %get-tuple-element.36), channel_id=1, source_target_pairs={{8,0},{16,8},{24,16},{0,24},{9,1},{17,9},{25,17},{1,25},{10,2},{18... | collective-permute-start | bytes 147464 | tf_op jit(solution)/shard_map/ppermute | solution.py:396
  7.3 0.7 %collective-permute-start = (bf16[16,12,128]{2,1,0:T(8,128)(2,1)S(1)}, bf16[16,12,128]{2,1,0:T(8,128)(2,1)S(1)}, u32[]{:S(2)}, u32[]{:S(2)}) collective-permute-start(bf16[16,12,128]{2,1,0:T(8,128)(2,1)S(1)} %get-tuple-element.34), channel_id=1, source_target_pairs={{1,2},{3,4},{5,6},{2,1},{4,3},{6,5},{9,10},{11,12},{13,14},{10,9},... | collective-permute-start | bytes 147464 | tf_op jit(solution)/shard_map/ppermute | solution.py:392
  7.9 3.1 %collective-permute-start.3 = (bf16[16,12,128]{2,1,0:T(8,128)(2,1)S(1)}, bf16[16,12,128]{2,1,0:T(8,128)(2,1)S(1)}, u32[]{:S(2)}, u32[]{:S(2)}) collective-permute-start(bf16[16,12,128]{2,1,0:T(8,128)(2,1)S(1)} %get-tuple-element.37), channel_id=1, source_target_pairs={{0,1},{2,3},{4,5},{6,7},{1,0},{3,2},{5,4},{7,6},{8,9},{10,11},{12,... | collective-permute-start | bytes 147464 | tf_op jit(solution)/shard_map/ppermute | solution.py:392
  11.7 0.0 copy-start.1
  11.7 1.5 %shard_map.119 = (f32[16,128]{1,0:T(8,128)S(1)}, f32[256,128]{1,0:T(8,128)S(1)}, bf16[256,256]{1,0:T(8,128)(2,1)S(1)}, bf16[256,256]{1,0:T(8,128)(2,1)S(1)}, bf1...) custom-call(s32[1,1]{1,0:T(1,128)} %bitcast.8.count_ref, ...), custom_call_target="tpu_custom_call" | custom-call | tf_op jit(solution)/shard_map/pallas_call | solution.py:436
  13.2 0.0 collective-permute-done.1.west_ref
  13.2 0.0 collective-permute-done.2.east_ref
  13.2 0.0 collective-permute-done.outer_ref
  13.2 0.0 collective-permute-done.3.inner_ref
  13.2 0.0 copy-start
  13.3 0.7 %shard_map.120 = (bf16[16,248,128]{2,1,0:T(8,128)(2,1)S(1)}, f32[16,4,16,128]{3,2,1,0:T(8,128)S(1)}) custom-call(f32[16,12,16,128]{3,2,1,0:T(8,128)S(1)} %get-tuple-element.33.inside_ref, bf16[16,12,128]{2,1,0:T(8,128)(2,1)S(1)} %collective-permute-done.outer_ref, bf16[12,16,128]{2,1,0:T(8,128)(2,1)S(1)} %collective-permute-done.1.west_ref, ...), custom_call_target="tpu_custom_call" | custom-call | tf_op jit(solution)/shard_map/pallas_call | solution.py:445
  14.0 30.0 %all_to_all.10.rows_ref = bf16[16,248,128]{2,1,0:T(8,128)(2,1)S(1)} all-to-all(bf16[16,248,128]{2,1,0:T(8,128)(2,1)S(1)} %get-tuple-element.42), channel_id=1, replica_groups=mesh['tile'=4,'lat'=4,'emu'=2] {'tile','lat'}, dimensions={0} | all-to-all | bytes 2031616 | tf_op jit(solution)/shard_map/all_to_all | solution.py:456
  44.0 0.0 copy-done.1
  44.0 0.0 copy-done
  44.0 3.2 %shard_map.121 = bf16[16,80,128]{2,1,0:T(8,128)(2,1)S(1)} custom-call(bf16[16,248,128]{2,1,0:T(8,128)(2,1)S(1)} %all_to_all.10.rows_ref, f32[1,1024]{1,0:T(1,128)S(1)} %get-tuple-element.43.b_first, f32[1,1024]{1,0:T(1,128)S(1)} %get-tuple-element.44.land_add, f32[2,1024]{1,0:T(2,128)S(1)} %get-tuple-element.45.b_inner, ...), custom_call_target="tpu_custom_call" | custom-call | tf_op jit(solution)/shard_map/pallas_call | solution.py:457
  47.2 14.2 %all_to_all.11.rows_ref = bf16[16,80,128]{2,1,0:T(8,128)(2,1)S(1)} all-to-all(bf16[16,80,128]{2,1,0:T(8,128)(2,1)S(1)} %shard_map.121), channel_id=1, replica_groups=mesh['tile'=4,'lat'=4,'emu'=2] {'tile','lat'}, dimensions={0} | all-to-all | bytes 655360 | tf_op jit(solution)/shard_map/all_to_all | solution.py:466
  61.4 1.1 %shard_map.122 = f32[1024,128]{1,0:T(8,128)} custom-call(bf16[16,80,128]{2,1,0:T(8,128)(2,1)S(1)} %all_to_all.11.rows_ref, f32[16,4,16,128]{3,2,1,0:T(8,128)S(1)} %get-tuple-element.48.kept_ref, bf16[256,256]{1,0:T(8,128)(2,1)S(1)} %get-tuple-element.49.refs_0_, bf16[256,256]{1,0:T(8,128)(2,1)S(1)} %get-tuple-element.50.refs_1_), custom_call_target="tpu_custom_call" | custom-call | tf_op jit(solution)/shard_map/pallas_call | solution.py:467
Async XLA Ops:
  2.1 11.1 %collective-permute-start.1 = (bf16[12,16,128]{2,1,0:T(8,128)(2,1)S(1)}, bf16[12,16,128]{2,1,0:T(8,128)(2,1)S(1)}, u32[]{:S(2)}, u32[]{:S(2)}) collective-permute-start(bf16[12,16,128]{2,1,0:T(8,128)(2,1)S(1)} %get-tuple-element.35), channel_id=1, source_target_pairs={{0,8},{8,16},{16,24},{24,0},{1,9},{9,17},{17,25},{25,1},{2,10},{10... | collective-permute-start | bytes 147464 | tf_op jit(solution)/shard_map/ppermute | solution.py:395
  5.2 8.0 %collective-permute-start.2 = (bf16[12,16,128]{2,1,0:T(8,128)(2,1)S(1)}, bf16[12,16,128]{2,1,0:T(8,128)(2,1)S(1)}, u32[]{:S(2)}, u32[]{:S(2)}) collective-permute-start(bf16[12,16,128]{2,1,0:T(8,128)(2,1)S(1)} %get-tuple-element.36), channel_id=1, source_target_pairs={{8,0},{16,8},{24,16},{0,24},{9,1},{17,9},{25,17},{1,25},{10,2},{18... | collective-permute-start | bytes 147464 | tf_op jit(solution)/shard_map/ppermute | solution.py:396
  7.3 6.0 %collective-permute-start = (bf16[16,12,128]{2,1,0:T(8,128)(2,1)S(1)}, bf16[16,12,128]{2,1,0:T(8,128)(2,1)S(1)}, u32[]{:S(2)}, u32[]{:S(2)}) collective-permute-start(bf16[16,12,128]{2,1,0:T(8,128)(2,1)S(1)} %get-tuple-element.34), channel_id=1, source_target_pairs={{1,2},{3,4},{5,6},{2,1},{4,3},{6,5},{9,10},{11,12},{13,14},{10,9},... | collective-permute-start | bytes 147464 | tf_op jit(solution)/shard_map/ppermute | solution.py:392
  7.9 5.3 %collective-permute-start.3 = (bf16[16,12,128]{2,1,0:T(8,128)(2,1)S(1)}, bf16[16,12,128]{2,1,0:T(8,128)(2,1)S(1)}, u32[]{:S(2)}, u32[]{:S(2)}) collective-permute-start(bf16[16,12,128]{2,1,0:T(8,128)(2,1)S(1)} %get-tuple-element.37), channel_id=1, source_target_pairs={{0,1},{2,3},{4,5},{6,7},{1,0},{3,2},{5,4},{7,6},{8,9},{10,11},{12,... | collective-permute-start | bytes 147464 | tf_op jit(solution)/shard_map/ppermute | solution.py:392
  11.7 32.3 %copy-start.1 = (bf16[1,1024,512]{2,1,0:T(8,128)(2,1)S(1)}, bf16[1,1024,512]{2,1,0:T(8,128)(2,1)}, u32[]{:S(2)}) copy-start(bf16[1,1024,512]{2,1,0:T(8,128)(2,1)} %param.23) | copy-start | bytes 3145732
  13.2 30.7 %copy-start = (bf16[1,2,1024,1024]{3,2,1,0:T(8,128)(2,1)S(1)}, bf16[1,2,1024,1024]{3,2,1,0:T(8,128)(2,1)}, u32[]{:S(2)}) copy-start(bf16[1,2,1024,1024]{3,2,1,0:T(8,128)(2,1)} %param.21) | copy-start | bytes 12582916

commit v7 on v6

--- a/solution.py
+++ b/solution.py
@@ -16,8 +16,10 @@
 
 
 class Plan:
-    def __init__(self, experts, capacity):
-        self.experts = experts
+    def __init__(self, tiles, bands, capacity):
+        self.experts = tiles * bands
+        middle = sorted(range(tiles), key=lambda tile: abs(2 * tile - tiles + 1))
+        self.order = [tile * bands + band for band in range(bands) for tile in middle]
         self.full = capacity // 16 * 16
         self.rest = capacity - self.full
         self.group = 8 // math.gcd(self.rest, 8) if self.rest else 1
@@ -77,7 +79,10 @@
     experts = plan.experts
     columns = routes_ref.shape[1]
     lons, lats = land_ref.shape
-    routes = routes_ref[...]
+    named = routes_ref[...]
+    routes = jnp.zeros_like(named)
+    for place, expert in enumerate(plan.order):
+        routes = jnp.where(named == expert, place, routes)
     active = iota((1, columns), 1) < count_ref[0, 0]
     owner = (iota((experts, columns), 0) == routes) & active
     owner_hot = hot(owner)
@@ -404,9 +409,10 @@
     lons, lats, variables, levels = state.shape
     columns = lons * lats
     outs = w_out.shape[2] // levels
-    experts = lax.axis_size("tile") * lax.axis_size("lat")
+    tiles, bands = lax.axis_size("tile"), lax.axis_size("lat")
+    experts = tiles * bands
     capacity = max(2, columns * 5 // (4 * experts))
-    plan = Plan(experts, capacity)
+    plan = Plan(tiles, bands, capacity)
     state = jnp.transpose(state, (0, 2, 1, 3))
     w_in = far(w_in[0])
     head = w_in.shape[0] // 2
@@ -452,8 +458,17 @@
         [pltpu.VMEM((columns, variables * levels), BF16)],
     )(inside, *halos, diffusivity, half_wind, flags, *packs)
 
-    axes = ("tile", "lat")
-    rows = lax.all_to_all(rows, axes, split_axis=0, concat_axis=0, tiled=True)
+    def exchange(values):
+        return lax.all_to_all(
+            values,
+            ("tile", "lat"),
+            split_axis=0,
+            concat_axis=0,
+            axis_index_groups=[plan.order],
+            tiled=True,
+        )
+
+    rows = exchange(rows)
     made = call(
         functools.partial(network_kernel, plan),
         [VM] * 8,
@@ -463,7 +478,7 @@
         ],
         16,
     )(rows, b_in, land_vec, b_hid, w_head, w_tail, w_hid[0], w_out[0])
-    made = lax.all_to_all(made, axes, split_axis=0, concat_axis=0, tiled=True)
+    made = exchange(made)
     out = call(
         functools.partial(finish_kernel, plan),
         [VM] * (2 + len(picks)),

time: 62.7 us -> 59.4 us (0.947)
  blocking collectives: 44.2 us -> 40.9 us
    all_to_all x2, blocking collectives: 44.2 us -> 40.9 us  [exchange(): lax.all_to_all(values, ('tile', 'lat'), split_axis=0, concat_axis=0, axis...]
  transfers between devices with their start and end apart: 4 -> 4, of which waited for: 0 -> 0; matrix products, arithmetic and copies ran while one was open for 0% -> 0% of each run, Pallas kernels for 2% -> 3%
where the time goes in v7:
time: 59.4 us; the launch traced here: 59.2 us
  blocking collectives  40.9 us (69%)
  starting transfers between devices  8.92 us (15%)
  Pallas kernels  8.61 us (14%)
  between operations  0.74 us (1%)
    all_to_all x2, blocking collectives, exchange(): lax.all_to_all(values, ('tile', 'lat'), split_axis=0, concat_axis=0, axis...  40.9 us
    ppermute x2, starting transfers between devices, swap(): lax.ppermute(values, ('lat', 'emu'), pairs + [(b, a) for a, b in pairs])  3.72 us
    pallas_call x1, Pallas kernels, body(): call(functools.partial(network_kernel, plan), [VM] * 8, shape((experts, p...  3.2 us
    ppermute x1, starting transfers between devices, exchanged(): west = lax.ppermute(top, 'tile', up)  3.1 us
    ppermute x1, starting transfers between devices, exchanged(): east = lax.ppermute(bottom, 'tile', [(b, a) for a, b in up])  2.09 us
    pallas_call x1, Pallas kernels, exchanged(): call(edge_kernel, [HB] * len(values), [shape(v.shape, v.dtype) for v in v...  2.07 us
    pallas_call x1, Pallas kernels, body(): call(functools.partial(route_kernel, plan), [SM, VM, VM, VM, VM, VM, HB],...  1.51 us
  transfers between devices with their start and end apart: 4, of which 0 were waited for; matrix products, arithmetic and copies ran while one was open for 0% of the time, Pallas kernels for 3%

profile of v7, /device:TPU:0, one launch (start us, length us, event | category | flops | bytes accessed | tf_op | source)
XLA Modules:
  0.0 59.2 jit_solution(13267296741517693768)
XLA Ops:
  0.0 2.1 %shard_map.118 = (f32[16,12,16,128]{3,2,1,0:T(8,128)S(1)}, f32[12,128]{1,0:T(8,128)S(1)}, f32[16,16]{1,0:T(8,128)S(1)}, s32[16,16]{1,0:T(8,128)S(1)}, s32[1,256]...) custom-call(f32[16,12,16,128]{3,2,1,0:T(8,128)} %bitcast.13, ...), custom_call_target="tpu_custom_call" | custom-call | tf_op jit(solution)/shard_map/pallas_call | solution.py:383
  2.1 3.1 %collective-permute-start.1 = (bf16[12,16,128]{2,1,0:T(8,128)(2,1)S(1)}, bf16[12,16,128]{2,1,0:T(8,128)(2,1)S(1)}, u32[]{:S(2)}, u32[]{:S(2)}) collective-permute-start(bf16[12,16,128]{2,1,0:T(8,128)(2,1)S(1)} %get-tuple-element.35), channel_id=1, source_target_pairs={{0,8},{8,16},{16,24},{24,0},{1,9},{9,17},{17,25},{25,1},{2,10},{10... | collective-permute-start | bytes 147464 | tf_op jit(solution)/shard_map/ppermute | solution.py:400
  5.2 2.1 %collective-permute-start.2 = (bf16[12,16,128]{2,1,0:T(8,128)(2,1)S(1)}, bf16[12,16,128]{2,1,0:T(8,128)(2,1)S(1)}, u32[]{:S(2)}, u32[]{:S(2)}) collective-permute-start(bf16[12,16,128]{2,1,0:T(8,128)(2,1)S(1)} %get-tuple-element.36), channel_id=1, source_target_pairs={{8,0},{16,8},{24,16},{0,24},{9,1},{17,9},{25,17},{1,25},{10,2},{18... | collective-permute-start | bytes 147464 | tf_op jit(solution)/shard_map/ppermute | solution.py:401
  7.3 0.7 %collective-permute-start = (bf16[16,12,128]{2,1,0:T(8,128)(2,1)S(1)}, bf16[16,12,128]{2,1,0:T(8,128)(2,1)S(1)}, u32[]{:S(2)}, u32[]{:S(2)}) collective-permute-start(bf16[16,12,128]{2,1,0:T(8,128)(2,1)S(1)} %get-tuple-element.34), channel_id=1, source_target_pairs={{1,2},{3,4},{5,6},{2,1},{4,3},{6,5},{9,10},{11,12},{13,14},{10,9},... | collective-permute-start | bytes 147464 | tf_op jit(solution)/shard_map/ppermute | solution.py:397
  7.9 3.1 %collective-permute-start.3 = (bf16[16,12,128]{2,1,0:T(8,128)(2,1)S(1)}, bf16[16,12,128]{2,1,0:T(8,128)(2,1)S(1)}, u32[]{:S(2)}, u32[]{:S(2)}) collective-permute-start(bf16[16,12,128]{2,1,0:T(8,128)(2,1)S(1)} %get-tuple-element.37), channel_id=1, source_target_pairs={{0,1},{2,3},{4,5},{6,7},{1,0},{3,2},{5,4},{7,6},{8,9},{10,11},{12,... | collective-permute-start | bytes 147464 | tf_op jit(solution)/shard_map/ppermute | solution.py:397
  11.7 0.0 copy-start.1
  11.7 1.5 %shard_map.119 = (f32[16,128]{1,0:T(8,128)S(1)}, f32[256,128]{1,0:T(8,128)S(1)}, bf16[256,256]{1,0:T(8,128)(2,1)S(1)}, bf16[256,256]{1,0:T(8,128)(2,1)S(1)}, bf1...) custom-call(s32[1,1]{1,0:T(1,128)} %bitcast.8.count_ref, ...), custom_call_target="tpu_custom_call" | custom-call | tf_op jit(solution)/shard_map/pallas_call | solution.py:442
  13.2 0.0 collective-permute-done.1.west_ref
  13.2 0.0 collective-permute-done.2.east_ref
  13.2 0.0 collective-permute-done.outer_ref
  13.2 0.0 collective-permute-done.3.inner_ref
  13.2 0.0 copy-start
  13.2 0.7 %shard_map.120 = (bf16[16,248,128]{2,1,0:T(8,128)(2,1)S(1)}, f32[16,4,16,128]{3,2,1,0:T(8,128)S(1)}) custom-call(f32[16,12,16,128]{3,2,1,0:T(8,128)S(1)} %get-tuple-element.33.inside_ref, bf16[16,12,128]{2,1,0:T(8,128)(2,1)S(1)} %collective-permute-done.outer_ref, bf16[12,16,128]{2,1,0:T(8,128)(2,1)S(1)} %collective-permute-done.1.west_ref, ...), custom_call_target="tpu_custom_call" | custom-call | tf_op jit(solution)/shard_map/pallas_call | solution.py:451
  14.0 28.8 %all_to_all.10.rows_ref = bf16[16,248,128]{2,1,0:T(8,128)(2,1)S(1)} all-to-all(bf16[16,248,128]{2,1,0:T(8,128)(2,1)S(1)} %get-tuple-element.42), channel_id=1, replica_groups={{8,16,0,24,10,18,2,26,12,20,4,28,14,22,6,30},{9,17,1,25,11,19,3,27,13,2..., dimensions={0} | all-to-all | bytes 2031616 | tf_op jit(solution)/shard_map/all_to_all | solution.py:462
  42.8 0.0 copy-done.1
  42.8 0.0 copy-done
  42.8 3.2 %shard_map.121 = bf16[16,80,128]{2,1,0:T(8,128)(2,1)S(1)} custom-call(bf16[16,248,128]{2,1,0:T(8,128)(2,1)S(1)} %all_to_all.10.rows_ref, f32[1,1024]{1,0:T(1,128)S(1)} %get-tuple-element.43.b_first, f32[1,1024]{1,0:T(1,128)S(1)} %get-tuple-element.44.land_add, f32[2,1024]{1,0:T(2,128)S(1)} %get-tuple-element.45.b_inner, ...), custom_call_target="tpu_custom_call" | custom-call | tf_op jit(solution)/shard_map/pallas_call | solution.py:472
  46.0 12.1 %all_to_all.11.rows_ref = bf16[16,80,128]{2,1,0:T(8,128)(2,1)S(1)} all-to-all(bf16[16,80,128]{2,1,0:T(8,128)(2,1)S(1)} %shard_map.121), channel_id=1, replica_groups={{8,16,0,24,10,18,2,26,12,20,4,28,14,22,6,30},{9,17,1,25,11,19,3,27,13,2..., dimensions={0} | all-to-all | bytes 655360 | tf_op jit(solution)/shard_map/all_to_all | solution.py:462
  58.1 1.1 %shard_map.122 = f32[1024,128]{1,0:T(8,128)} custom-call(bf16[16,80,128]{2,1,0:T(8,128)(2,1)S(1)} %all_to_all.11.rows_ref, f32[16,4,16,128]{3,2,1,0:T(8,128)S(1)} %get-tuple-element.48.kept_ref, bf16[256,256]{1,0:T(8,128)(2,1)S(1)} %get-tuple-element.49.refs_0_, bf16[256,256]{1,0:T(8,128)(2,1)S(1)} %get-tuple-element.50.refs_1_), custom_call_target="tpu_custom_call" | custom-call | tf_op jit(solution)/shard_map/pallas_call | solution.py:482
Async XLA Ops:
  2.1 11.1 %collective-permute-start.1 = (bf16[12,16,128]{2,1,0:T(8,128)(2,1)S(1)}, bf16[12,16,128]{2,1,0:T(8,128)(2,1)S(1)}, u32[]{:S(2)}, u32[]{:S(2)}) collective-permute-start(bf16[12,16,128]{2,1,0:T(8,128)(2,1)S(1)} %get-tuple-element.35), channel_id=1, source_target_pairs={{0,8},{8,16},{16,24},{24,0},{1,9},{9,17},{17,25},{25,1},{2,10},{10... | collective-permute-start | bytes 147464 | tf_op jit(solution)/shard_map/ppermute | solution.py:400
  5.2 8.0 %collective-permute-start.2 = (bf16[12,16,128]{2,1,0:T(8,128)(2,1)S(1)}, bf16[12,16,128]{2,1,0:T(8,128)(2,1)S(1)}, u32[]{:S(2)}, u32[]{:S(2)}) collective-permute-start(bf16[12,16,128]{2,1,0:T(8,128)(2,1)S(1)} %get-tuple-element.36), channel_id=1, source_target_pairs={{8,0},{16,8},{24,16},{0,24},{9,1},{17,9},{25,17},{1,25},{10,2},{18... | collective-permute-start | bytes 147464 | tf_op jit(solution)/shard_map/ppermute | solution.py:401
  7.3 5.9 %collective-permute-start = (bf16[16,12,128]{2,1,0:T(8,128)(2,1)S(1)}, bf16[16,12,128]{2,1,0:T(8,128)(2,1)S(1)}, u32[]{:S(2)}, u32[]{:S(2)}) collective-permute-start(bf16[16,12,128]{2,1,0:T(8,128)(2,1)S(1)} %get-tuple-element.34), channel_id=1, source_target_pairs={{1,2},{3,4},{5,6},{2,1},{4,3},{6,5},{9,10},{11,12},{13,14},{10,9},... | collective-permute-start | bytes 147464 | tf_op jit(solution)/shard_map/ppermute | solution.py:397
  7.9 5.3 %collective-permute-start.3 = (bf16[16,12,128]{2,1,0:T(8,128)(2,1)S(1)}, bf16[16,12,128]{2,1,0:T(8,128)(2,1)S(1)}, u32[]{:S(2)}, u32[]{:S(2)}) collective-permute-start(bf16[16,12,128]{2,1,0:T(8,128)(2,1)S(1)} %get-tuple-element.37), channel_id=1, source_target_pairs={{0,1},{2,3},{4,5},{6,7},{1,0},{3,2},{5,4},{7,6},{8,9},{10,11},{12,... | collective-permute-start | bytes 147464 | tf_op jit(solution)/shard_map/ppermute | solution.py:397
  11.7 31.2 %copy-start.1 = (bf16[1,1024,512]{2,1,0:T(8,128)(2,1)S(1)}, bf16[1,1024,512]{2,1,0:T(8,128)(2,1)}, u32[]{:S(2)}) copy-start(bf16[1,1024,512]{2,1,0:T(8,128)(2,1)} %param.23) | copy-start | bytes 3145732
  13.2 29.6 %copy-start = (bf16[1,2,1024,1024]{3,2,1,0:T(8,128)(2,1)S(1)}, bf16[1,2,1024,1024]{3,2,1,0:T(8,128)(2,1)}, u32[]{:S(2)}) copy-start(bf16[1,2,1024,1024]{3,2,1,0:T(8,128)(2,1)} %param.21) | copy-start | bytes 12582916
